TPU v7x, 128 devices: a whole 4x4x4 slice. The times are simulated.
128 devices in a mesh: sta: 8 (over x, y_hi), gx: 4 (over z), gy: 4 (over y_lo, core).
Axes of the slice: x: 4, y: 4 (y_hi: 2, y_lo: 2; y = y_hi * 2 + y_lo), z: 4, core: 2. Of those that a mesh axis runs over, the one named last changes fastest.
Arguments:
- rec_state: float32 [8, 4, 9, 32, 32, 128], P('sta', None, None, 'gx', 'gy'), may hold values from -6 to 6
- source_strain: bfloat16 [8, 8, 6, 32, 32, 128], P('sta', None, None, 'gx', 'gy'), may hold values from -6 to 6
- material: int32 [32, 32, 128], P('gx', 'gy'), may hold values from 0 to 15
- material_table: float32 [16, 3], replicated, may hold values from 0.5 to 1.5
- residual: float32 [8, 4, 8], P('sta'), may hold values from -4 to 4
- rec_cell: int32 [8, 4], P('sta'), may hold values from 0 to 1023
- listed: int32 [2, 8, 8], replicated, may hold values 0 or 1
- src_pick: int32 [2, 8], replicated, may hold values from 0 to 7
Outputs:
- kernels: float32 [2, 32, 32, 128], P(None, ('gx', 'sta'), 'gy')
All inputs are finite; a program needn't handle non-finite values.
Results may differ from a plain program's by a relative error of at most 0.0003.
Values may be sent and summed in bfloat16 or wider, within the bound.
A program may use at most 128 MiB of HBM per device.

v0:
```python
import jax
import jax.numpy as jnp
from jax import lax
from jax.sharding import PartitionSpec as P

C_NEAR = 8.0 / 12.0
C_FAR = -1.0 / 12.0
TIME_STEP = 0.25
AMPLITUDE = 4.0
KERNEL_SCALE = 0.0625
STIFFNESS = 0.3


def with_halo(block, sides, width):
    for axis, dim in sides:
        count = lax.axis_size(axis)
        forward = [(i, i + 1) for i in range(count - 1)]
        backward = [(target, source) for source, target in forward]
        low = lax.ppermute(
            lax.slice_in_dim(block, block.shape[dim] - width, None, axis=dim), axis, forward
        )
        high = lax.ppermute(lax.slice_in_dim(block, 0, width, axis=dim), axis, backward)
        block = jnp.concatenate([low, block, high], axis=dim)
    return block


def from_root(block, axis, source):
    block = jnp.where(lax.axis_index(axis) == source, block, jnp.zeros_like(block))
    return lax.psum(block, axis)


def along_first(padded):
    core = padded[..., :, 2:-2, 2:-2]
    return C_NEAR * (core[..., 3:-1, :, :] - core[..., 1:-3, :, :]) + C_FAR * (
        core[..., 4:, :, :] - core[..., :-4, :, :]
    )


def along_second(padded):
    core = padded[..., 2:-2, :, 2:-2]
    return C_NEAR * (core[..., :, 3:-1, :] - core[..., :, 1:-3, :]) + C_FAR * (
        core[..., :, 4:, :] - core[..., :, :-4, :]
    )


def along_depth(padded):
    core = padded[..., 2:-2, 2:-2, :]
    return C_NEAR * (core[..., 3:-1] - core[..., 1:-3]) + C_FAR * (core[..., 4:] - core[..., :-4])


def pad_depth(field):
    return jnp.pad(field, [(0, 0)] * (field.ndim - 1) + [(2, 2)])


def force_terms(padded, source_term):
    first = along_first(padded[:, 0]) + along_second(padded[:, 3]) + along_depth(padded[:, 4])
    second = along_first(padded[:, 3]) + along_second(padded[:, 1]) + along_depth(padded[:, 5])
    third = (
        along_first(padded[:, 4])
        + along_second(padded[:, 5])
        + along_depth(padded[:, 2])
        + source_term
    )
    return jnp.stack([first, second, third], 1)


def strain_rates(padded):
    comp_first = padded[:, 0]
    comp_second = padded[:, 1]
    comp_depth = padded[:, 2]
    rate_first = along_first(comp_first)
    rate_second = along_second(comp_second)
    rate_depth = along_depth(comp_depth)
    shear_plane = 0.5 * (along_second(comp_first) + along_first(comp_second))
    shear_first = 0.5 * (along_depth(comp_first) + along_first(comp_depth))
    shear_second = 0.5 * (along_depth(comp_second) + along_second(comp_depth))
    return jnp.stack(
        [rate_first, rate_second, rate_depth, shear_plane, shear_first, shear_second], 1
    )


def update_stress(stress, rates, lame, shear):
    trace = rates[:, 0] + rates[:, 1] + rates[:, 2]
    diagonal = stress[:, :3] + TIME_STEP * (lame * trace[:, None] + 2.0 * shear * rates[:, :3])
    offdiag = stress[:, 3:] + TIME_STEP * (2.0 * shear * rates[:, 3:])
    return jnp.concatenate([diagonal, offdiag], 1)


def correlate(source, weighted):
    trace_src = source[0] + source[1] + source[2]
    trace_rec = weighted[0] + weighted[1] + weighted[2]
    lam_part = trace_src * trace_rec
    diag_part = source[0] * weighted[0] + source[1] * weighted[1] + source[2] * weighted[2]
    off_part = source[3] * weighted[3] + source[4] * weighted[4] + source[5] * weighted[5]
    return jnp.stack([lam_part, 2.0 * diag_part + 4.0 * off_part])


def local(rec_state, source_strain, material, material_table, residual, rec_cell, listed, src_pick):
    state = rec_state[0]
    tile_x = state.shape[2]
    tile_y = state.shape[3]
    depth = state.shape[4]
    group = lax.axis_index("sta")
    count_mat = material_table.shape[0]
    onehot = (material[None] == jnp.arange(count_mat, dtype=jnp.int32)[:, None, None, None]).astype(
        jnp.float32
    )
    props = jnp.einsum("kxyz,kc->cxyz", onehot, material_table, precision=lax.Precision.HIGHEST)
    buoyancy = TIME_STEP / props[0]
    lame = STIFFNESS * props[1]
    shear = STIFFNESS * props[2]
    depth_first = (jnp.arange(depth) == 0).astype(jnp.float32)
    row_index = lax.axis_index("gx") * tile_x + jnp.arange(tile_x, dtype=jnp.int32)
    col_index = lax.axis_index("gy") * tile_y + jnp.arange(tile_y, dtype=jnp.int32)
    ny_total = lax.axis_size("gy") * tile_y
    cells = rec_cell[0]
    spots = ((cells // ny_total)[:, None, None] == row_index[None, :, None]) & (
        (cells % ny_total)[:, None, None] == col_index[None, None, :]
    )
    spots = spots.astype(jnp.float32)
    res_rows = residual[0]
    velocity = state[:, :3]
    stress = state[:, 3:]
    aggregates = []
    for moment in range(res_rows.shape[1]):
        source_term = (
            (AMPLITUDE * res_rows[:, moment])[:, None, None, None]
            * spots[:, :, :, None]
            * depth_first
        )
        stress_pad = pad_depth(with_halo(stress, (("gx", 2), ("gy", 3)), 2))
        velocity = velocity + buoyancy * force_terms(stress_pad, source_term)
        velocity_pad = pad_depth(with_halo(velocity, (("gx", 2), ("gy", 3)), 2))
        rates = strain_rates(velocity_pad)
        stress = update_stress(stress, rates, lame, shear)
        aggregates.append(
            jnp.sum((KERNEL_SCALE * res_rows[:, moment])[:, None, None, None, None] * rates, 0)
        )
    weights = lax.dynamic_slice_in_dim(listed, group, 1, 2)[:, :, 0].astype(jnp.float32)
    kernel = jnp.zeros((2, tile_x, tile_y, depth), jnp.float32)
    for rounds in range(listed.shape[0]):
        for moment in range(len(aggregates)):
            snaps = from_root(source_strain[0, moment], "sta", src_pick[rounds, moment])
            kernel = kernel + weights[rounds, moment] * correlate(
                snaps.astype(jnp.float32), aggregates[moment]
            )
    total = lax.psum(kernel, "sta")
    share = tile_x // lax.axis_size("sta")
    return lax.dynamic_slice_in_dim(total, group * share, share, 1)


def solution(mesh):
    in_specs = (
        P("sta", None, None, "gx", "gy", None),
        P("sta", None, None, "gx", "gy", None),
        P("gx", "gy", None),
        P(),
        P("sta", None, None),
        P("sta", None),
        P(),
        P(),
    )
    out_specs = P(None, ("gx", "sta"), "gy", None)
    return jax.shard_map(local, mesh=mesh, in_specs=in_specs, out_specs=out_specs, check_vma=False)
```

profile of v0, /device:TPU:0, one launch (start us, length us, event | category | flops | bytes accessed | tf_op | source)
XLA Modules:
  0.0 574.8 jit_solution(6821561108950658713)
XLA Ops:
  41.9 5.5 collective-permute-start.6
  62.2 4.4 collective-permute-done.9
  85.8 4.3 collective-permute-done.13
  90.2 5.5 collective-permute-start.14
  108.8 4.4 collective-permute-done.17
  132.1 4.3 collective-permute-done.21
  136.5 5.5 collective-permute-start.22
  155.1 4.4 collective-permute-done.25
  178.4 4.3 collective-permute-done.29
  182.8 5.5 collective-permute-start.30
  201.4 4.4 collective-permute-done.33
  220.3 5.5 select_maximum_fusion.15
  252.6 4.5 collective-permute-start.40
  265.7 5.3 collective-permute-start.42
  274.1 73.0 %all-reduce.22.cloned.1.call-done = (bf16[6,8,8,128]{3,2,1,0:T(8,128)(2,1)}, bf16[6,8,8,128]{3,2,1,0:T(8,128)(2,1)}, bf16[6,8,8,128]{3,2,1,0:T(8,128)(2,1)}, bf1...) async-done(((bf16[6,8,8,128]{3,2,1,0:T(8,128)(2,1)}, ...) | async-done | bytes 1572880 | tf_op jit(solution)/shard_map/psum | solution.py:29
  349.0 5.8 %select_maximum_fusion.10 = f32[4,6,12,12,132]{4,3,2,0,1:T(8,128)S(1)} fusion(f32[4,6,12,2,128]{4,3,2,0,1:T(2,128)} %collective-permute-done.43, f32[4,6,12,2,128]{4,3,2,0,1:T(2,128)} %collective-permute-done.42, f32[4,6,2,8,128]{4,3,2,0,1:T(8,128)} %copy-done.20, f32[4,6,2,8,128]{4,3,2,0,1:T(8,128)S(1)} %collective-permute-done.40, ...), kind=kLoop, calls=%fused_computation.14 | loop fusion | flops 6386688 | bytes 3594240 | tf_op jit(solution)/shard_map/concatenate | solution.py:23
  363.3 4.3 collective-permute-done.45
  382.3 4.5 collective-permute-done.49
  407.1 4.3 collective-permute-done.53
  411.5 5.5 collective-permute-start.54
  429.4 4.4 collective-permute-done.57
  457.3 5.5 collective-permute-start.62
  470.4 10.8 %fusion.647 = f32[2,8,8,128]{3,2,1,0:T(8,128)} fusion(f32[1,8,8,128]{3,2,1,0:T(8,128)S(1)} %get-tuple-element.290, f32[1,8,8,128]{3,2,1,0:T(8,128)S(1)} %get-tuple-element.289, f32[1,8,8,128]{3,2,1,0:T(8,128)S(1)} %get-tuple-element.286, f32[1,8,8,128]{3,2,1,0:T(8,128)S(1)} %get-tuple-element.285, f32[1,8,8,128]{3,2,1,0:T(8,128)S(1)} %get-tuple-element.282, ...), kind=kLoop, calls=%fused_computation.1256 | loop fusion | flops 770048 | bytes 1114176 | tf_op jit(solution)/shard_map/add | solution.py:144
  481.3 84.9 %all-reduce.20.cloned.1.call-done = f32[2,8,8,128]{3,2,1,0:T(8,128)} async-done(((f32[2,8,8,128]{3,2,1,0:T(8,128)}), f32[2,8,8,128]{3,2,1,0:T(8,128)}) %all-reduce.20.cloned.1.call-update) | async-done | bytes 65552 | tf_op jit(solution)/shard_map/psum | solution.py:147
  (434 shorter events, 276.9 us)
Async XLA Ops:
  6.5 340.5 %all-reduce.22.cloned.1.call-start = ((), (), s32[]{:S(2)}) async-start(), calls=%async_computation.1 | async-start | bytes 3145728 | tf_op jit(solution)/shard_map/psum | solution.py:29
  7.7 9.9 %collective-permute-start = (f32[4,6,2,8,128]{4,3,2,0,1:T(8,128)S(1)}, f32[4,6,2,8,128]{4,3,2,0,1:T(8,128)S(1)}, u32[]{:S(2)}, u32[]{:S(2)}) collective-permute-start(f32[4,6,2,8,128]{4,3,2,0,1:T(8,128)S(1)} %copy.59), channel_id=1, source_target_pairs={{0,4},{4,8},{8,12},{1,5},{5,9},{9,13},{2,6},{6,10},{10,14},{3,7},{... | collective-permute-start | bytes 589832 | tf_op jit(solution)/shard_map/ppermute | solution.py:19
  11.7 8.4 %collective-permute-start.1 = (f32[4,6,2,8,128]{4,3,2,0,1:T(8,128)S(1)}, f32[4,6,2,8,128]{4,3,2,0,1:T(8,128)S(1)}, u32[]{:S(2)}, u32[]{:S(2)}) collective-permute-start(f32[4,6,2,8,128]{4,3,2,0,1:T(8,128)S(1)} %copy.61), channel_id=1, source_target_pairs={{4,0},{8,4},{12,8},{5,1},{9,5},{13,9},{6,2},{10,6},{14,10},{7,3},{... | collective-permute-start | bytes 589832 | tf_op jit(solution)/shard_map/ppermute | solution.py:22
  41.9 6.9 %collective-permute-start.6 = (f32[4,3,12,2,128]{4,3,2,0,1:T(2,128)S(1)}, f32[4,3,12,2,128]{4,3,2,0,1:T(2,128)S(1)}, u32[]{:S(2)}, u32[]{:S(2)}) collective-permute-start(f32[4,3,12,2,128]{4,3,2,0,1:T(2,128)S(1)} %get-tuple-element.243), channel_id=1, source_target_pairs={{0,1},{1,2},{2,3},{4,5},{5,6},{6,7},{8,9},{9,10},{10,11},{12,13},{... | collective-permute-start | bytes 442376 | tf_op jit(solution)/shard_map/ppermute | solution.py:19
  59.0 7.6 %collective-permute-start.9 = (f32[4,6,2,8,128]{4,3,2,0,1:T(8,128)S(1)}, f32[4,6,2,8,128]{4,3,2,0,1:T(8,128)S(1)}, u32[]{:S(2)}, u32[]{:S(2)}) collective-permute-start(f32[4,6,2,8,128]{4,3,2,0,1:T(8,128)S(1)} %get-tuple-element.212), channel_id=1, source_target_pairs={{4,0},{8,4},{12,8},{5,1},{9,5},{13,9},{6,2},{10,6},{14,10},{7,3},{... | collective-permute-start | bytes 589832 | tf_op jit(solution)/shard_map/ppermute | solution.py:22
  90.2 6.9 %collective-permute-start.14 = (f32[4,3,12,2,128]{4,3,2,0,1:T(2,128)S(1)}, f32[4,3,12,2,128]{4,3,2,0,1:T(2,128)S(1)}, u32[]{:S(2)}, u32[]{:S(2)}) collective-permute-start(f32[4,3,12,2,128]{4,3,2,0,1:T(2,128)S(1)} %get-tuple-element.241), channel_id=1, source_target_pairs={{0,1},{1,2},{2,3},{4,5},{5,6},{6,7},{8,9},{9,10},{10,11},{12,13},{... | collective-permute-start | bytes 442376 | tf_op jit(solution)/shard_map/ppermute | solution.py:19
  105.7 7.6 %collective-permute-start.17 = (f32[4,6,2,8,128]{4,3,2,0,1:T(8,128)S(1)}, f32[4,6,2,8,128]{4,3,2,0,1:T(8,128)S(1)}, u32[]{:S(2)}, u32[]{:S(2)}) collective-permute-start(f32[4,6,2,8,128]{4,3,2,0,1:T(8,128)S(1)} %get-tuple-element.210), channel_id=1, source_target_pairs={{4,0},{8,4},{12,8},{5,1},{9,5},{13,9},{6,2},{10,6},{14,10},{7,3},{... | collective-permute-start | bytes 589832 | tf_op jit(solution)/shard_map/ppermute | solution.py:22
  136.5 6.9 %collective-permute-start.22 = (f32[4,3,12,2,128]{4,3,2,0,1:T(2,128)S(1)}, f32[4,3,12,2,128]{4,3,2,0,1:T(2,128)S(1)}, u32[]{:S(2)}, u32[]{:S(2)}) collective-permute-start(f32[4,3,12,2,128]{4,3,2,0,1:T(2,128)S(1)} %get-tuple-element.239), channel_id=1, source_target_pairs={{0,1},{1,2},{2,3},{4,5},{5,6},{6,7},{8,9},{9,10},{10,11},{12,13},{... | collective-permute-start | bytes 442376 | tf_op jit(solution)/shard_map/ppermute | solution.py:19
  151.9 7.6 %collective-permute-start.25 = (f32[4,6,2,8,128]{4,3,2,0,1:T(8,128)S(1)}, f32[4,6,2,8,128]{4,3,2,0,1:T(8,128)S(1)}, u32[]{:S(2)}, u32[]{:S(2)}) collective-permute-start(f32[4,6,2,8,128]{4,3,2,0,1:T(8,128)S(1)} %get-tuple-element.208), channel_id=1, source_target_pairs={{4,0},{8,4},{12,8},{5,1},{9,5},{13,9},{6,2},{10,6},{14,10},{7,3},{... | collective-permute-start | bytes 589832 | tf_op jit(solution)/shard_map/ppermute | solution.py:22
  182.8 6.9 %collective-permute-start.30 = (f32[4,3,12,2,128]{4,3,2,0,1:T(2,128)S(1)}, f32[4,3,12,2,128]{4,3,2,0,1:T(2,128)S(1)}, u32[]{:S(2)}, u32[]{:S(2)}) collective-permute-start(f32[4,3,12,2,128]{4,3,2,0,1:T(2,128)S(1)} %get-tuple-element.237), channel_id=1, source_target_pairs={{0,1},{1,2},{2,3},{4,5},{5,6},{6,7},{8,9},{9,10},{10,11},{12,13},{... | collective-permute-start | bytes 442376 | tf_op jit(solution)/shard_map/ppermute | solution.py:19
  198.2 7.6 %collective-permute-start.33 = (f32[4,6,2,8,128]{4,3,2,0,1:T(8,128)S(1)}, f32[4,6,2,8,128]{4,3,2,0,1:T(8,128)S(1)}, u32[]{:S(2)}, u32[]{:S(2)}) collective-permute-start(f32[4,6,2,8,128]{4,3,2,0,1:T(8,128)S(1)} %get-tuple-element.206), channel_id=1, source_target_pairs={{4,0},{8,4},{12,8},{5,1},{9,5},{13,9},{6,2},{10,6},{14,10},{7,3},{... | collective-permute-start | bytes 589832 | tf_op jit(solution)/shard_map/ppermute | solution.py:22
  206.8 13.4 %collective-permute-start.34 = (f32[4,6,12,2,128]{4,3,2,0,1:T(2,128)}, f32[4,6,12,2,128]{4,3,2,0,1:T(2,128)S(1)}, u32[]{:S(2)}, u32[]{:S(2)}) collective-permute-start(f32[4,6,12,2,128]{4,3,2,0,1:T(2,128)} %get-tuple-element.185), channel_id=1, source_target_pairs={{0,1},{1,2},{2,3},{4,5},{5,6},{6,7},{8,9},{9,10},{10,11},{12,13},{... | collective-permute-start | bytes 884744 | tf_op jit(solution)/shard_map/ppermute | solution.py:19
  211.0 9.3 %collective-permute-start.35 = (f32[4,6,12,2,128]{4,3,2,0,1:T(2,128)}, f32[4,6,12,2,128]{4,3,2,0,1:T(2,128)}, u32[]{:S(2)}, u32[]{:S(2)}) collective-permute-start(f32[4,6,12,2,128]{4,3,2,0,1:T(2,128)} %get-tuple-element.186), channel_id=1, source_target_pairs={{1,0},{2,1},{3,2},{5,4},{6,5},{7,6},{9,8},{10,9},{11,10},{13,12},{... | collective-permute-start | bytes 884744 | tf_op jit(solution)/shard_map/ppermute | solution.py:22
  228.9 8.8 %collective-permute-start.36 = (f32[4,3,2,8,128]{4,3,2,0,1:T(8,128)}, f32[4,3,2,8,128]{4,3,2,0,1:T(8,128)S(1)}, u32[]{:S(2)}, u32[]{:S(2)}) collective-permute-start(f32[4,3,2,8,128]{4,3,2,0,1:T(8,128)} %get-tuple-element.275), channel_id=1, source_target_pairs={{0,4},{4,8},{8,12},{1,5},{5,9},{9,13},{2,6},{6,10},{10,14},{3,7},{... | collective-permute-start | bytes 294920 | tf_op jit(solution)/shard_map/ppermute | solution.py:19
  231.1 7.2 %collective-permute-start.37 = (f32[4,3,2,8,128]{4,3,2,0,1:T(8,128)S(1)}, f32[4,3,2,8,128]{4,3,2,0,1:T(8,128)S(1)}, u32[]{:S(2)}, u32[]{:S(2)}) collective-permute-start(f32[4,3,2,8,128]{4,3,2,0,1:T(8,128)S(1)} %get-tuple-element.276), channel_id=1, source_target_pairs={{4,0},{8,4},{12,8},{5,1},{9,5},{13,9},{6,2},{10,6},{14,10},{7,3},{... | collective-permute-start | bytes 294920 | tf_op jit(solution)/shard_map/ppermute | solution.py:22
  245.9 320.3 %all-reduce.20.cloned.1.call-start = ((), (), s32[]{:S(2)}) async-start(), calls=%async_computation | async-start | bytes 131072 | tf_op jit(solution)/shard_map/psum | solution.py:147
  252.6 8.0 %collective-permute-start.40 = (f32[4,6,2,8,128]{4,3,2,0,1:T(8,128)}, f32[4,6,2,8,128]{4,3,2,0,1:T(8,128)S(1)}, u32[]{:S(2)}, u32[]{:S(2)}) collective-permute-start(f32[4,6,2,8,128]{4,3,2,0,1:T(8,128)} %get-tuple-element.203), channel_id=1, source_target_pairs={{0,4},{4,8},{8,12},{1,5},{5,9},{9,13},{2,6},{6,10},{10,14},{3,7},{... | collective-permute-start | bytes 589832 | tf_op jit(solution)/shard_map/ppermute | solution.py:19
  257.1 7.6 %collective-permute-start.41 = (f32[4,6,2,8,128]{4,3,2,0,1:T(8,128)S(1)}, f32[4,6,2,8,128]{4,3,2,0,1:T(8,128)S(1)}, u32[]{:S(2)}, u32[]{:S(2)}) collective-permute-start(f32[4,6,2,8,128]{4,3,2,0,1:T(8,128)S(1)} %get-tuple-element.204), channel_id=1, source_target_pairs={{4,0},{8,4},{12,8},{5,1},{9,5},{13,9},{6,2},{10,6},{14,10},{7,3},{... | collective-permute-start | bytes 589832 | tf_op jit(solution)/shard_map/ppermute | solution.py:22
  265.7 83.3 %collective-permute-start.42 = (f32[4,6,12,2,128]{4,3,2,0,1:T(2,128)}, f32[4,6,12,2,128]{4,3,2,0,1:T(2,128)}, u32[]{:S(2)}, u32[]{:S(2)}) collective-permute-start(f32[4,6,12,2,128]{4,3,2,0,1:T(2,128)} %get-tuple-element.183), channel_id=1, source_target_pairs={{0,1},{1,2},{2,3},{4,5},{5,6},{6,7},{8,9},{9,10},{10,11},{12,13},{... | collective-permute-start | bytes 884744 | tf_op jit(solution)/shard_map/ppermute | solution.py:19
  270.9 78.0 %collective-permute-start.43 = (f32[4,6,12,2,128]{4,3,2,0,1:T(2,128)}, f32[4,6,12,2,128]{4,3,2,0,1:T(2,128)}, u32[]{:S(2)}, u32[]{:S(2)}) collective-permute-start(f32[4,6,12,2,128]{4,3,2,0,1:T(2,128)} %get-tuple-element.184), channel_id=1, source_target_pairs={{1,0},{2,1},{3,2},{5,4},{6,5},{7,6},{9,8},{10,9},{11,10},{13,12},{... | collective-permute-start | bytes 884744 | tf_op jit(solution)/shard_map/ppermute | solution.py:22
  379.2 7.6 %collective-permute-start.49 = (f32[4,6,2,8,128]{4,3,2,0,1:T(8,128)S(1)}, f32[4,6,2,8,128]{4,3,2,0,1:T(8,128)S(1)}, u32[]{:S(2)}, u32[]{:S(2)}) collective-permute-start(f32[4,6,2,8,128]{4,3,2,0,1:T(8,128)S(1)} %get-tuple-element.202), channel_id=1, source_target_pairs={{4,0},{8,4},{12,8},{5,1},{9,5},{13,9},{6,2},{10,6},{14,10},{7,3},{... | collective-permute-start | bytes 589832 | tf_op jit(solution)/shard_map/ppermute | solution.py:22
  411.5 6.9 %collective-permute-start.54 = (f32[4,3,12,2,128]{4,3,2,0,1:T(2,128)S(1)}, f32[4,3,12,2,128]{4,3,2,0,1:T(2,128)S(1)}, u32[]{:S(2)}, u32[]{:S(2)}) collective-permute-start(f32[4,3,12,2,128]{4,3,2,0,1:T(2,128)S(1)} %get-tuple-element.231), channel_id=1, source_target_pairs={{0,1},{1,2},{2,3},{4,5},{5,6},{6,7},{8,9},{9,10},{10,11},{12,13},{... | collective-permute-start | bytes 442376 | tf_op jit(solution)/shard_map/ppermute | solution.py:19
  426.3 7.6 %collective-permute-start.57 = (f32[4,6,2,8,128]{4,3,2,1,0:T(8,128)S(1)}, f32[4,6,2,8,128]{4,3,2,1,0:T(8,128)S(1)}, u32[]{:S(2)}, u32[]{:S(2)}) collective-permute-start(f32[4,6,2,8,128]{4,3,2,1,0:T(8,128)S(1)} %get-tuple-element.200), channel_id=1, source_target_pairs={{4,0},{8,4},{12,8},{5,1},{9,5},{13,9},{6,2},{10,6},{14,10},{7,3},{... | collective-permute-start | bytes 589832 | tf_op jit(solution)/shard_map/ppermute | solution.py:22
  457.3 6.9 %collective-permute-start.62 = (f32[4,3,12,2,128]{4,3,2,0,1:T(2,128)S(1)}, f32[4,3,12,2,128]{4,3,2,0,1:T(2,128)S(1)}, u32[]{:S(2)}, u32[]{:S(2)}) collective-permute-start(f32[4,3,12,2,128]{4,3,2,0,1:T(2,128)S(1)} %get-tuple-element.229), channel_id=1, source_target_pairs={{0,1},{1,2},{2,3},{4,5},{5,6},{6,7},{8,9},{9,10},{10,11},{12,13},{... | collective-permute-start | bytes 442376 | tf_op jit(solution)/shard_map/ppermute | solution.py:19
  (92 other events, 809.4 us)
Sparse Core Ops, SparseCore 0:
  246.0 101.0 all-reduce.21
  481.4 84.7 all-reduce.19
where the time goes:
time: 585 us; the launch traced here: 575 us
  waiting for transfers between devices  275 us (47%)
  starting transfers between devices  157 us (27%)
  other arithmetic  96.7 us (17%)
  between operations  26.7 us (5%)
  local copies, waits for them, and re-layouts  18.2 us (3%)
    ppermute x32, starting transfers between devices, with_halo(): lax.ppermute(lax.slice_in_dim(block, block.shape[dim] - width, None, axis...  114 us
    ppermute x32, waiting for transfers between devices, with_halo(): lax.ppermute(lax.slice_in_dim(block, 0, width, axis=dim), axis, backward)  99.5 us
    psum x1, waiting for transfers between devices, local(): total = lax.psum(kernel, 'sta')  84.9 us
    psum x1, waiting for transfers between devices, from_root(): return lax.psum(block, axis)  73 us
    concatenate x16, other arithmetic, with_halo(): block = jnp.concatenate([low, block, high], axis=dim)  43.9 us
    ppermute x32, starting transfers between devices, with_halo(): lax.ppermute(lax.slice_in_dim(block, 0, width, axis=dim), axis, backward)  43.2 us
    ppermute x32, waiting for transfers between devices, with_halo(): lax.ppermute(lax.slice_in_dim(block, block.shape[dim] - width, None, axis...  17.8 us
  transfers between devices with their start and end apart: 66, of which 46 were waited for; matrix products, arithmetic and copies ran while one was open for 4% of the time, Pallas kernels for 0%

commit v1 on v0

v1 whole, which is shorter than its diff:
```python
import functools

import jax
import jax.numpy as jnp
from jax import lax
from jax.experimental import pallas as pl
from jax.experimental.pallas import tpu as pltpu
from jax.sharding import PartitionSpec as P

MESH = pl.DeviceIdType.MESH
F32 = jnp.float32
BF16 = jnp.bfloat16

C_NEAR = 8.0 / 12.0
TIME_STEP = 0.25
AMPLITUDE = 4.0
KERNEL_SCALE = 0.0625
STIFFNESS = 0.3

YY, YZ, XY, XX, XZ, ZZ = range(6)
STRESS_FROM = (1, 5, 3, 0, 4, 2)
VX, VY, VZ = range(3)
SIDES = (("gx", -1), ("gx", 1), ("gy", -1), ("gy", 1))
XLO, XHI, YLO, YHI = range(4)


def body(
    rec_hbm,
    src_hbm,
    mat_hbm,
    table_ref,
    res_ref,
    cell_ref,
    listed_ref,
    pick_ref,
    out_ref,
    stress,
    stress_y,
    vel,
    vel_y,
    weighted,
    mat,
    coef,
    rows_in,
    mine,
    other,
    gath,
    acc,
    parts,
    in_sem,
    h_send,
    h_recv,
    a_send,
    a_recv,
    b_sem,
    g_send,
    g_recv,
    r_send,
    r_recv,
):
    recs = stress.shape[0]
    steps = weighted.shape[0]
    tile_x = coef.shape[1]
    rows, depth = coef.shape[2], coef.shape[3]
    turns = listed_ref.shape[0]
    n_sta = parts.shape[0]
    n_col = gath.shape[0]
    gx, gy, sta = lax.axis_index("gx"), lax.axis_index("gy"), lax.axis_index("sta")
    n_gx, n_gy = lax.axis_size("gx"), lax.axis_size("gy")
    sx, sy = sta // 2, sta % 2
    pos = {"gx": (gx, n_gx), "gy": (gy, n_gy)}

    loads = [pltpu.make_async_copy(mat_hbm, mat, in_sem.at[0])]
    for c, src in enumerate(STRESS_FROM):
        loads.append(
            pltpu.make_async_copy(
                rec_hbm.at[0, :, 3 + src], stress.at[:, c, pl.ds(2, tile_x)], in_sem.at[1 + c]
            )
        )
    for c in range(3):
        loads.append(
            pltpu.make_async_copy(
                rec_hbm.at[0, :, c], vel.at[:, c, pl.ds(2, tile_x)], in_sem.at[7 + c]
            )
        )
    own_rows = pltpu.make_async_copy(
        src_hbm.at[0, :, :, pl.ds(2 * sx, 2)], rows_in.at[sx], in_sem.at[10]
    )
    for load in loads:
        load.start()
    own_rows.start()

    zero = jnp.zeros((rows, depth), F32)

    @pl.loop(0, recs)
    def _(r):
        for c in range(6):
            for row in (0, 1, tile_x + 2, tile_x + 3):
                stress[r, c, row] = zero
        for c in range(3):
            for row in (0, 1, tile_x + 2, tile_x + 3):
                vel[r, c, row] = zero
            for row in range(tile_x):
                stress_y[r, c, row] = zero
                vel_y[r, c, row] = zero

    barrier = pltpu.get_barrier_semaphore()

    def has(side):
        axis, step = SIDES[side]
        at, count = pos[axis]
        return at > 0 if step < 0 else at < count - 1

    for d in range(1, n_sta):
        pl.semaphore_signal(
            barrier, inc=1, device_id={"sta": (sta + d) % n_sta}, device_id_type=MESH
        )
    for side, (axis, step) in enumerate(SIDES):

        @pl.when(has(side))
        def _(axis=axis, step=step):
            pl.semaphore_signal(
                barrier, inc=1, device_id={axis: pos[axis][0] + step}, device_id_type=MESH
            )

    loads[0].wait()
    for x in range(tile_x):
        m = mat[x]
        b = jnp.zeros((rows, depth), F32)
        la = jnp.zeros((rows, depth), F32)
        sh = jnp.zeros((rows, depth), F32)
        for k in range(table_ref.shape[0]):
            hit = m == k
            b = jnp.where(hit, table_ref[k, 0], b)
            la = jnp.where(hit, table_ref[k, 1], la)
            sh = jnp.where(hit, table_ref[k, 2], sh)
        coef[0, x] = TIME_STEP * C_NEAR / b
        coef[1, x] = (TIME_STEP * STIFFNESS * C_NEAR) * la
        coef[2, x] = (TIME_STEP * STIFFNESS * C_NEAR) * sh

    @pl.loop(0, steps)
    def _(n):
        for c in range(6):
            for x in range(tile_x):
                weighted[n, c, x] = zero

    for load in loads[1:]:
        load.wait()
    peers = n_sta - 1
    for side in range(4):
        peers = peers + has(side).astype(jnp.int32)
    pl.semaphore_wait(barrier, peers)

    def halo(kind, side, r):
        axis, step = SIDES[side]
        at, count = pos[axis]
        to = jnp.clip(at + step, 0, count - 1)
        field, edge = ((stress, stress_y), (vel, vel_y))[kind]
        if axis == "gx":
            cs = pl.ds(XY if kind == 0 else 0, 3)
            src = field.at[r, cs, pl.ds(2 if step < 0 else tile_x, 2)]
            dst = field.at[r, cs, pl.ds(tile_x + 2 if step < 0 else 0, 2)]
        else:
            at_row = pl.ds(0 if step < 0 else rows - 2, 2)
            src = field.at[r, pl.ds(0, 3), pl.ds(2, tile_x), at_row]
            dst = edge.at[r, :, :, at_row]
        return pltpu.make_async_remote_copy(
            src_ref=src,
            dst_ref=dst,
            send_sem=h_send.at[kind, side, r],
            recv_sem=h_recv.at[kind, side, r],
            device_id={axis: to},
            device_id_type=MESH,
        )

    def send(kind, r):
        for side in range(4):

            @pl.when(has(side))
            def _(side=side):
                halo(kind, side, r).start()

    def arrive(kind, r):
        for side in range(4):

            @pl.when(has(side ^ 1))
            def _(side=side):
                halo(kind, side, r).wait_recv()

            @pl.when(has(side))
            def _(side=side):
                halo(kind, side, r).wait_send()

    @pl.loop(0, recs)
    def _(r):
        send(0, r)

    def row_copy(d):
        to = (sx + d) % n_col
        return pltpu.make_async_remote_copy(
            src_ref=src_hbm.at[0, :, :, pl.ds(2 * to, 2)],
            dst_ref=rows_in.at[sx],
            send_sem=a_send.at[d - 1],
            recv_sem=a_recv.at[d - 1],
            device_id={"sta": 2 * to + sy},
            device_id_type=MESH,
        )

    for d in range(1, n_col):
        row_copy(d).start()

    partner_copy = pltpu.make_async_remote_copy(
        src_ref=mine,
        dst_ref=other,
        send_sem=b_sem.at[0],
        recv_sem=b_sem.at[1],
        device_id={"sta": 2 * sx + 1 - sy},
        device_id_type=MESH,
    )

    def ring(k):
        step = 1 if k % 2 == 0 else n_col - 1
        to = (sx + step) % n_col
        slot = sx if k < 2 else (sx + n_col - step) % n_col
        part = pl.ds(0, turns * steps) if k < 2 else pl.ds((k - 2) * steps, steps)
        ref = gath.at[slot, part]
        return pltpu.make_async_remote_copy(
            src_ref=ref,
            dst_ref=ref,
            send_sem=g_send.at[k],
            recv_sem=g_recv.at[k],
            device_id={"sta": 2 * to + sy},
            device_id_type=MESH,
        )

    def pick_rows():
        own_rows.wait()
        for d in range(1, n_col):
            row_copy(d).wait()
        for t in range(turns):

            @pl.loop(0, steps)
            def _(n, t=t):
                p = pick_ref[t, n]
                keep = p % 2 == sy
                for c in range(6):
                    for j in range(2):
                        v = rows_in[p // 2, n, c, j]
                        mine[t * steps + n, c, j] = jnp.where(keep, v, jnp.zeros_like(v))

        partner_copy.start()

    def gather_rows():
        partner_copy.wait()

        @pl.loop(0, turns * steps)
        def _(q):
            for c in range(6):
                for j in range(2):
                    gath[sx, q, c, j] = mine[q, c, j] + other[q, c, j]

        ring(0).start()
        ring(1).start()

    def relay_rows():
        ring(0).wait()
        ring(1).wait()
        ring(2).start()
        ring(3).start()

    row_at = lax.broadcasted_iota(jnp.int32, (rows, depth), 0)
    lane_at = lax.broadcasted_iota(jnp.int32, (rows, depth), 1)
    first1, first2 = row_at < 1, row_at < 2
    last1, last2 = row_at >= rows - 1, row_at >= rows - 2
    src_at = lax.broadcasted_iota(jnp.int32, (2 * depth, depth), 0) % depth
    off = src_at - lax.broadcasted_iota(jnp.int32, (2 * depth, depth), 1)
    band = jnp.where(off == 1, 1.0, 0.0) - jnp.where(off == -1, 1.0, 0.0)
    band = band + 0.125 * (jnp.where(off == -2, 1.0, 0.0) - jnp.where(off == 2, 1.0, 0.0))
    band = band.astype(BF16)

    def diff_x(ref, r, c, x):
        near = ref[r, c, x + 3] - ref[r, c, x + 1]
        return near - 0.125 * (ref[r, c, x + 4] - ref[r, c, x])

    def diff_y(ref, edge, r, c, x):
        t, e = ref[r, c, x + 2], edge[r, c, x]
        up1 = pltpu.roll(jnp.where(first1, e, t), rows - 1, 0)
        up2 = pltpu.roll(jnp.where(first2, e, t), rows - 2, 0)
        dn1 = pltpu.roll(jnp.where(last1, e, t), 1, 0)
        dn2 = pltpu.roll(jnp.where(last2, e, t), 2, 0)
        return (up1 - dn1) - 0.125 * (up2 - dn2)

    def diff_z(ref, r, c):
        f = ref[r, c, pl.ds(2, tile_x)].reshape(tile_x * rows, depth)
        hi = f.astype(BF16)
        lo = (f - hi.astype(F32)).astype(BF16)
        both = jnp.concatenate([hi, lo], 1)
        d = jnp.dot(both, band, preferred_element_type=F32)
        return d.reshape(tile_x, rows, depth)

    def velocity(n, r):
        zx = diff_z(stress, r, XZ)
        zy = diff_z(stress, r, YZ)
        zz = diff_z(stress, r, ZZ)
        cell = cell_ref[0, r]
        cx = cell // (n_gy * rows) - gx * tile_x
        cy = cell % (n_gy * rows) - gy * rows
        amp = (AMPLITUDE / C_NEAR) * res_ref[0, r, n]
        spot = jnp.where((row_at == cy) & (lane_at == 0), amp, 0.0)
        for x in range(tile_x):
            b = coef[0, x]
            fx = diff_x(stress, r, XX, x) + diff_y(stress, stress_y, r, XY, x) + zx[x]
            fy = diff_x(stress, r, XY, x) + diff_y(stress, stress_y, r, YY, x) + zy[x]
            fz = diff_x(stress, r, XZ, x) + diff_y(stress, stress_y, r, YZ, x) + zz[x]
            fz = fz + spot * jnp.where(cx == x, 1.0, 0.0)
            vel[r, VX, x + 2] = vel[r, VX, x + 2] + b * fx
            vel[r, VY, x + 2] = vel[r, VY, x + 2] + b * fy
            vel[r, VZ, x + 2] = vel[r, VZ, x + 2] + b * fz

    def strain(n, r):
        zx = diff_z(vel, r, VX)
        zy = diff_z(vel, r, VY)
        zz = diff_z(vel, r, VZ)
        res = res_ref[0, r, n]
        for x in range(tile_x):
            la, mu = coef[1, x], coef[2, x]
            mu2 = mu + mu
            rxx = diff_x(vel, r, VX, x)
            ryy = diff_y(vel, vel_y, r, VY, x)
            rzz = zz[x]
            rxy = diff_y(vel, vel_y, r, VX, x) + diff_x(vel, r, VY, x)
            rxz = zx[x] + diff_x(vel, r, VZ, x)
            ryz = zy[x] + diff_y(vel, vel_y, r, VZ, x)
            tr = la * (rxx + ryy + rzz)
            put = ((XX, rxx), (YY, ryy), (ZZ, rzz), (XY, rxy), (XZ, rxz), (YZ, ryz))
            for k, (c, v) in enumerate(put):
                weighted[n, k, x] = weighted[n, k, x] + res * v
                if k < 3:
                    stress[r, c, x + 2] = stress[r, c, x + 2] + (tr + mu2 * v)
                else:
                    stress[r, c, x + 2] = stress[r, c, x + 2] + mu * v

    @pl.loop(0, steps)
    def _(n):
        @pl.loop(0, recs)
        def _(r):
            arrive(0, r)
            velocity(n, r)
            send(1, r)

        @pl.loop(0, recs)
        def _(r):
            arrive(1, r)
            strain(n, r)

            @pl.when(n < steps - 1)
            def _():
                send(0, r)

        pl.when(n == 2)(pick_rows)
        pl.when(n == 4)(gather_rows)
        pl.when(n == 6)(relay_rows)

    ring(2).wait()
    ring(3).wait()

    for x in range(tile_x):
        for k in range(2):
            acc[x, k] = zero

    scale = KERNEL_SCALE * C_NEAR

    @pl.loop(0, steps)
    def _(n):
        share = [listed_ref[t, n, sta].astype(F32) for t in range(turns)]
        for x in range(tile_x):
            comb = []
            for c in range(6):
                total = None
                for t in range(turns):
                    v = share[t] * gath[x // 2, t * steps + n, c, x % 2].astype(F32)
                    total = v if total is None else total + v
                comb.append(total)
            w = [weighted[n, k, x] for k in range(6)]
            lam = (comb[0] + comb[1] + comb[2]) * (w[0] + w[1] + w[2])
            mu = comb[0] * w[0]
            for c in range(1, 6):
                mu = mu + comb[c] * w[c]
            acc[x, 0] = acc[x, 0] + scale * lam
            acc[x, 1] = acc[x, 1] + (2.0 * scale) * mu

    def share_copy(d):
        to = (sta + d) % n_sta
        return pltpu.make_async_remote_copy(
            src_ref=acc.at[to],
            dst_ref=parts.at[d],
            send_sem=r_send.at[d],
            recv_sem=r_recv.at[d],
            device_id={"sta": to},
            device_id_type=MESH,
        )

    for d in range(1, n_sta):
        share_copy(d).start()
    for k in range(2):
        out_ref[k, 0] = acc[sta, k]
    for d in range(1, n_sta):
        share_copy(d).wait()
        for k in range(2):
            out_ref[k, 0] = out_ref[k, 0] + parts[d, k]


def local(rec_state, source_strain, material, material_table, residual, rec_cell, listed, src_pick):
    _, recs, _, tile_x, tile_y, depth = rec_state.shape
    steps = source_strain.shape[1]
    turns = listed.shape[0]
    n_sta = lax.axis_size("sta")
    n_col = n_sta // 2
    plane = (tile_y, depth)
    any_ = pl.BlockSpec(memory_space=pl.ANY)
    smem = pl.BlockSpec(memory_space=pltpu.SMEM)
    dma = pltpu.SemaphoreType.DMA
    return pl.pallas_call(
        body,
        out_shape=jax.ShapeDtypeStruct((2, 1, *plane), F32),
        in_specs=[any_, any_, any_, smem, smem, smem, smem, smem],
        out_specs=pl.BlockSpec(memory_space=pltpu.VMEM),
        scratch_shapes=[
            pltpu.VMEM((recs, 6, tile_x + 4, *plane), F32),
            pltpu.VMEM((recs, 3, tile_x, *plane), F32),
            pltpu.VMEM((recs, 3, tile_x + 4, *plane), F32),
            pltpu.VMEM((recs, 3, tile_x, *plane), F32),
            pltpu.VMEM((steps, 6, tile_x, *plane), F32),
            pltpu.VMEM((tile_x, *plane), jnp.int32),
            pltpu.VMEM((3, tile_x, *plane), F32),
            pltpu.VMEM((n_col, steps, 6, 2, *plane), BF16),
            pltpu.VMEM((turns * steps, 6, 2, *plane), BF16),
            pltpu.VMEM((turns * steps, 6, 2, *plane), BF16),
            pltpu.VMEM((n_col, turns * steps, 6, 2, *plane), BF16),
            pltpu.VMEM((tile_x, 2, *plane), F32),
            pltpu.VMEM((n_sta, 2, *plane), F32),
            dma((11,)),
            dma((2, 4, recs)),
            dma((2, 4, recs)),
            dma((n_col - 1,)),
            dma((n_col - 1,)),
            dma((2,)),
            dma((4,)),
            dma((4,)),
            dma((n_sta,)),
            dma((n_sta,)),
        ],
        compiler_params=pltpu.CompilerParams(
            collective_id=0, has_side_effects=True, vmem_limit_bytes=48 << 20
        ),
        name="kernels",
    )(rec_state, source_strain, material, material_table, residual, rec_cell, listed, src_pick)


def solution(mesh):
    in_specs = (
        P("sta", None, None, "gx", "gy", None),
        P("sta", None, None, "gx", "gy", None),
        P("gx", "gy", None),
        P(),
        P("sta", None, None),
        P("sta", None),
        P(),
        P(),
    )
    out_specs = P(None, ("gx", "sta"), "gy", None)
    return jax.shard_map(local, mesh=mesh, in_specs=in_specs, out_specs=out_specs, check_vma=False)
```

time: 585 us -> 79.4 us (0.14); the launches traced: 575 us -> 78.5 us
  waiting for transfers between devices: 275 us -> 0 us
  starting transfers between devices: 157 us -> 0 us
  other arithmetic: 96.7 us -> 0 us
  Pallas kernels: 0 us -> 71.3 us
  between operations: 26.7 us -> 0.02 us
  local copies, waits for them, and re-layouts: 18.2 us -> 7.23 us
    psum x2 -> x0, waiting for transfers between devices: 158 us -> none  [the longest x1 84.9 us: local(): total = lax.psum(kernel, 'sta')]
    ppermute x64 -> x0, starting transfers between devices: 157 us -> none  [the longest x32 114 us: with_halo(): lax.ppermute(lax.slice_in_dim(block, block.shape[dim] - width, None, axis...]
    ppermute x64 -> x0, waiting for transfers between devices: 117 us -> none  [the longest x32 99.5 us: with_halo(): lax.ppermute(lax.slice_in_dim(block, 0, width, axis=dim), axis, backward)]
    pallas_call x0 -> x1, Pallas kernels: none -> 71.3 us  [local(): pl.pallas_call(body, out_shape=jax.ShapeDtypeStruct((2, 1, *plane), F32),...]
    concatenate x16 -> x0, other arithmetic: 43.9 us -> none  [with_halo(): block = jnp.concatenate([low, block, high], axis=dim)]
    add x25 -> x0, other arithmetic: 13.7 us -> none  [the longest x1 10.8 us: local(): kernel + weights[rounds, moment] * correlate(snaps.astype(jnp.float32), a...]
    another operation x32 -> x0, other arithmetic: 13.4 us -> none  [the longest x24 10.9 us: force_terms(): return jnp.stack([first, second, third], 1)]
    squeeze x16 -> x0, local copies, waits for them, and re-layouts: 7.97 us -> none  [the longest x8 6.15 us: force_terms(): padded[:, 0]]
  transfers between devices with their start and end apart: 66 -> 0, of which waited for: 46 -> 0; matrix products, arithmetic and copies ran while one was open for 4% -> 0% of each run, Pallas kernels for 0% -> 0%
where the time goes in v1:
time: 79.4 us; the launch traced here: 78.5 us
  Pallas kernels  71.3 us (90%)
  local copies, waits for them, and re-layouts  7.23 us (9%)
    pallas_call x1, Pallas kernels, local(): pl.pallas_call(body, out_shape=jax.ShapeDtypeStruct((2, 1, *plane), F32),...  71.3 us
    unnamed x16, local copies, waits for them, and re-layouts  7.23 us

profile of v1, /device:TPU:0, one launch (start us, length us, event | category | flops | bytes accessed | tf_op | source)
XLA Modules:
  0.0 78.5 jit_solution(16920367785463909397)
XLA Ops:
  0.0 0.8 copy.9.table_ref
  0.8 0.0 copy-start
  0.8 1.3 %copy-done = f32[1,4,9,8,8,128]{5,4,3,2,1,0:T(8,128)S(1)} copy-done((f32[1,4,9,8,8,128]{5,4,3,2,1,0:T(8,128)S(1)}, f32[1,4,9,8,8,128]{5,4,3,2,1,0:T(8,128)}, u32[]{:S(2)}) %copy-start) | copy-done | bytes 1179672
  2.0 0.0 copy-start.1
  2.0 1.1 %copy-done.1 = bf16[1,8,6,8,8,128]{5,4,3,2,1,0:T(8,128)(2,1)S(1)} copy-done((bf16[1,8,6,8,8,128]{5,4,3,2,1,0:T(8,128)(2,1)S(1)}, bf16[1,8,6,8,8,128]{5,4,3,2,1,0:T(8,128)(2,1)}, u32[]{:S(2)}) %copy-start.1) | copy-done | bytes 786456
  3.2 0.0 copy-start.2
  3.2 0.8 copy-done.2
  3.9 0.0 copy-start.3
  3.9 0.7 copy-done.3
  4.6 0.0 copy-start.4
  4.6 0.7 copy-done.4
  5.3 0.0 copy-start.5
  5.3 0.7 copy-done.5
  6.0 0.0 copy-start.6
  6.0 0.7 copy-done.6
  6.6 71.3 %kernels.1 = f32[2,1,8,128]{3,2,1,0:T(8,128)S(1)} custom-call(f32[1,4,9,8,8,128]{5,4,3,2,1,0:T(8,128)S(1)} %copy-done, bf16[1,8,6,8,8,128]{5,4,3,2,1,0:T(8,128)(2,1)S(1)} %copy-done.1, s32[8,8,128]{2,1,0:T(8,128)S(1)} %copy-done.2, f32[16,3]{1,0:T(8,128)S(1)} %copy.9.table_ref, f32[1,4,8]{2,1,0:T(4,128)S(1)} %copy-done.4, s32[1,4]{1,0:T(1,128)S(1)} %copy-done.6, ...), custom_call_target="tpu_custom_call" | custom-call | tf_op jit(solution)/shard_map/kernels/pallas_call | solution.py:423
  77.9 0.6 copy.11
Async XLA Ops:
  0.8 1.3 %copy-start = (f32[1,4,9,8,8,128]{5,4,3,2,1,0:T(8,128)S(1)}, f32[1,4,9,8,8,128]{5,4,3,2,1,0:T(8,128)}, u32[]{:S(2)}) copy-start(f32[1,4,9,8,8,128]{5,4,3,2,1,0:T(8,128)} %rec_hbm.1) | copy-start | bytes 3538948
  2.0 1.1 %copy-start.1 = (bf16[1,8,6,8,8,128]{5,4,3,2,1,0:T(8,128)(2,1)S(1)}, bf16[1,8,6,8,8,128]{5,4,3,2,1,0:T(8,128)(2,1)}, u32[]{:S(2)}) copy-start(bf16[1,8,6,8,8,128]{5,4,3,2,1,0:T(8,128)(2,1)} %src_hbm.1) | copy-start | bytes 2359300
  3.2 0.8 copy-start.2
  3.9 0.7 copy-start.3
  4.6 0.7 copy-start.4
  5.3 0.7 copy-start.5
  6.0 0.7 copy-start.6

commit v2 on v1

--- a/solution.py
+++ b/solution.py
@@ -28,11 +28,11 @@
     rec_hbm,
     src_hbm,
     mat_hbm,
-    table_ref,
-    res_ref,
-    cell_ref,
-    listed_ref,
-    pick_ref,
+    table_hbm,
+    res_hbm,
+    cell_hbm,
+    listed_hbm,
+    pick_hbm,
     out_ref,
     stress,
     stress_y,
@@ -47,6 +47,11 @@
     gath,
     acc,
     parts,
+    table_ref,
+    res_ref,
+    cell_ref,
+    listed_ref,
+    pick_ref,
     in_sem,
     h_send,
     h_recv,
@@ -86,6 +91,15 @@
     own_rows = pltpu.make_async_copy(
         src_hbm.at[0, :, :, pl.ds(2 * sx, 2)], rows_in.at[sx], in_sem.at[10]
     )
+    smalls = (
+        (table_hbm, table_ref),
+        (res_hbm, res_ref),
+        (cell_hbm, cell_ref),
+        (listed_hbm, listed_ref),
+        (pick_hbm, pick_ref),
+    )
+    for k, (a, b) in enumerate(smalls):
+        loads.insert(1 + k, pltpu.make_async_copy(a, b, in_sem.at[11 + k]))
     for load in loads:
         load.start()
     own_rows.start()
@@ -123,17 +137,18 @@
                 barrier, inc=1, device_id={axis: pos[axis][0] + step}, device_id_type=MESH
             )
 
-    loads[0].wait()
+    for load in loads[:6]:
+        load.wait()
     for x in range(tile_x):
         m = mat[x]
         b = jnp.zeros((rows, depth), F32)
         la = jnp.zeros((rows, depth), F32)
         sh = jnp.zeros((rows, depth), F32)
-        for k in range(table_ref.shape[0]):
+        for k in range(table_ref.shape[1]):
             hit = m == k
-            b = jnp.where(hit, table_ref[k, 0], b)
-            la = jnp.where(hit, table_ref[k, 1], la)
-            sh = jnp.where(hit, table_ref[k, 2], sh)
+            b = jnp.where(hit, table_ref[0, k], b)
+            la = jnp.where(hit, table_ref[1, k], la)
+            sh = jnp.where(hit, table_ref[2, k], sh)
         coef[0, x] = TIME_STEP * C_NEAR / b
         coef[1, x] = (TIME_STEP * STIFFNESS * C_NEAR) * la
         coef[2, x] = (TIME_STEP * STIFFNESS * C_NEAR) * sh
@@ -144,7 +159,7 @@
             for x in range(tile_x):
                 weighted[n, c, x] = zero
 
-    for load in loads[1:]:
+    for load in loads[6:]:
         load.wait()
     peers = n_sta - 1
     for side in range(4):
@@ -417,13 +432,14 @@
     n_sta = lax.axis_size("sta")
     n_col = n_sta // 2
     plane = (tile_y, depth)
-    any_ = pl.BlockSpec(memory_space=pl.ANY)
-    smem = pl.BlockSpec(memory_space=pltpu.SMEM)
+    hbm = pl.BlockSpec(memory_space=pltpu.HBM)
+    table = material_table.T
+    smalls = (table, residual, rec_cell, listed, src_pick)
     dma = pltpu.SemaphoreType.DMA
     return pl.pallas_call(
         body,
         out_shape=jax.ShapeDtypeStruct((2, 1, *plane), F32),
-        in_specs=[any_, any_, any_, smem, smem, smem, smem, smem],
+        in_specs=[hbm] * 8,
         out_specs=pl.BlockSpec(memory_space=pltpu.VMEM),
         scratch_shapes=[
             pltpu.VMEM((recs, 6, tile_x + 4, *plane), F32),
@@ -439,7 +455,8 @@
             pltpu.VMEM((n_col, turns * steps, 6, 2, *plane), BF16),
             pltpu.VMEM((tile_x, 2, *plane), F32),
             pltpu.VMEM((n_sta, 2, *plane), F32),
-            dma((11,)),
+            *[pltpu.SMEM(a.shape, a.dtype) for a in smalls],
+            dma((16,)),
             dma((2, 4, recs)),
             dma((2, 4, recs)),
             dma((n_col - 1,)),
@@ -451,10 +468,10 @@
             dma((n_sta,)),
         ],
         compiler_params=pltpu.CompilerParams(
-            collective_id=0, has_side_effects=True, vmem_limit_bytes=48 << 20
+            collective_id=0, has_side_effects=True
         ),
         name="kernels",
-    )(rec_state, source_strain, material, material_table, residual, rec_cell, listed, src_pick)
+    )(rec_state, source_strain, material, *smalls)
 
 
 def solution(mesh):

time: 79.4 us -> 72.8 us (0.917)
  local copies, waits for them, and re-layouts: 7.23 us -> 1.3 us
  Pallas kernels: 71.3 us -> 70.4 us
    unnamed x16 -> x1, local copies, waits for them, and re-layouts: 7.23 us -> 1.3 us
    pallas_call x1, Pallas kernels: 71.3 us -> 70.4 us  [local(): pl.pallas_call(body, out_shape=jax.ShapeDtypeStruct((2, 1, *plane), F32),...]
where the time goes in v2:
time: 72.8 us; the launch traced here: 71.7 us
  Pallas kernels  70.4 us (97%)
  local copies, waits for them, and re-layouts  1.3 us (2%)
    pallas_call x1, Pallas kernels, local(): pl.pallas_call(body, out_shape=jax.ShapeDtypeStruct((2, 1, *plane), F32),...  70.4 us

profile of v2, /device:TPU:0, one launch (start us, length us, event | category | flops | bytes accessed | tf_op | source)
XLA Modules:
  0.0 71.7 jit_solution(16729546086856711132)
XLA Ops:
  0.0 70.4 %kernels.1 = f32[2,1,8,128]{3,2,1,0:T(8,128)} custom-call(f32[1,4,9,8,8,128]{5,4,3,2,1,0:T(8,128)} %rec_hbm.1, bf16[1,8,6,8,8,128]{5,4,3,2,1,0:T(8,128)(2,1)} %src_hbm.1, s32[8,8,128]{2,1,0:T(8,128)} %mat_hbm.1, f32[3,16]{1,0:T(4,128)} %bitcast.1, f32[1,4,8]{2,1,0:T(4,128)} %res_hbm.1, s32[1,4]{1,0:T(1,128)} %cell_hbm.1, s32[2,8,8]{2,1,0:T(8,128)} %listed_hbm.1, ...), custom_call_target="tpu_custom_call" | custom-call | tf_op jit(solution)/shard_map/kernels/pallas_call | solution.py:439
  70.4 1.3 %copy.10 = f32[2,1,8,128]{3,2,1,0:T(8,128)} copy(f32[2,1,8,128]{3,2,1,0:T(8,128)} %kernels.1) | data formatting | bytes 16384

commit v3 on v2

--- a/solution.py
+++ b/solution.py
@@ -20,8 +20,8 @@
 YY, YZ, XY, XX, XZ, ZZ = range(6)
 STRESS_FROM = (1, 5, 3, 0, 4, 2)
 VX, VY, VZ = range(3)
-SIDES = (("gx", -1), ("gx", 1), ("gy", -1), ("gy", 1))
-XLO, XHI, YLO, YHI = range(4)
+WAYS = ((-1, 0), (1, 0), (0, -1), (0, 1), (-1, -1), (-1, 1), (1, -1), (1, 1))
+BACK = (1, 0, 3, 2, 7, 6, 5, 4)
 
 
 def body(
@@ -40,7 +40,9 @@
     vel_y,
     weighted,
     mat,
+    mat_y,
     coef,
+    coef_y,
     rows_in,
     mine,
     other,
@@ -53,6 +55,10 @@
     listed_ref,
     pick_ref,
     in_sem,
+    m_send,
+    m_recv,
+    i_send,
+    i_recv,
     h_send,
     h_recv,
     a_send,
@@ -65,17 +71,15 @@
 ):
     recs = stress.shape[0]
     steps = weighted.shape[0]
-    tile_x = coef.shape[1]
-    rows, depth = coef.shape[2], coef.shape[3]
+    tile_x, rows, depth = coef_y.shape[1:]
     turns = listed_ref.shape[0]
     n_sta = parts.shape[0]
     n_col = gath.shape[0]
     gx, gy, sta = lax.axis_index("gx"), lax.axis_index("gy"), lax.axis_index("sta")
     n_gx, n_gy = lax.axis_size("gx"), lax.axis_size("gy")
     sx, sy = sta // 2, sta % 2
-    pos = {"gx": (gx, n_gx), "gy": (gy, n_gy)}
-
-    loads = [pltpu.make_async_copy(mat_hbm, mat, in_sem.at[0])]
+
+    loads = [pltpu.make_async_copy(mat_hbm, mat.at[pl.ds(2, tile_x)], in_sem.at[0])]
     for c, src in enumerate(STRESS_FROM):
         loads.append(
             pltpu.make_async_copy(
@@ -85,7 +89,7 @@
     for c in range(3):
         loads.append(
             pltpu.make_async_copy(
-                rec_hbm.at[0, :, c], vel.at[:, c, pl.ds(2, tile_x)], in_sem.at[7 + c]
+                rec_hbm.at[0, :, c], vel.at[1, :, c, pl.ds(4, tile_x)], in_sem.at[7 + c]
             )
         )
     own_rows = pltpu.make_async_copy(
@@ -105,6 +109,11 @@
     own_rows.start()
 
     zero = jnp.zeros((rows, depth), F32)
+    none = jnp.full((rows, depth), -1, jnp.int32)
+    for row in (0, 1, tile_x + 2, tile_x + 3):
+        mat[row] = none
+    for row in range(tile_x):
+        mat_y[row] = none
 
     @pl.loop(0, recs)
     def _(r):
@@ -112,46 +121,42 @@
             for row in (0, 1, tile_x + 2, tile_x + 3):
                 stress[r, c, row] = zero
         for c in range(3):
-            for row in (0, 1, tile_x + 2, tile_x + 3):
-                vel[r, c, row] = zero
             for row in range(tile_x):
                 stress_y[r, c, row] = zero
-                vel_y[r, c, row] = zero
+            for p in range(2):
+                for row in range(4):
+                    vel[p, r, c, row] = zero
+                    vel[p, r, c, tile_x + 4 + row] = zero
+                for row in range(tile_x + 4):
+                    vel_y[p, r, c, row] = zero
 
     barrier = pltpu.get_barrier_semaphore()
 
-    def has(side):
-        axis, step = SIDES[side]
-        at, count = pos[axis]
-        return at > 0 if step < 0 else at < count - 1
+    def has(way):
+        dx, dy = WAYS[way]
+        ok = None
+        for d, at, count in ((dx, gx, n_gx), (dy, gy, n_gy)):
+            if d:
+                one = at > 0 if d < 0 else at < count - 1
+                ok = one if ok is None else ok & one
+        return ok
+
+    def device(way):
+        dx, dy = WAYS[way]
+        return {"gx": jnp.clip(gx + dx, 0, n_gx - 1), "gy": jnp.clip(gy + dy, 0, n_gy - 1)}
 
     for d in range(1, n_sta):
         pl.semaphore_signal(
             barrier, inc=1, device_id={"sta": (sta + d) % n_sta}, device_id_type=MESH
         )
-    for side, (axis, step) in enumerate(SIDES):
-
-        @pl.when(has(side))
-        def _(axis=axis, step=step):
-            pl.semaphore_signal(
-                barrier, inc=1, device_id={axis: pos[axis][0] + step}, device_id_type=MESH
-            )
-
-    for load in loads[:6]:
-        load.wait()
-    for x in range(tile_x):
-        m = mat[x]
-        b = jnp.zeros((rows, depth), F32)
-        la = jnp.zeros((rows, depth), F32)
-        sh = jnp.zeros((rows, depth), F32)
-        for k in range(table_ref.shape[1]):
-            hit = m == k
-            b = jnp.where(hit, table_ref[0, k], b)
-            la = jnp.where(hit, table_ref[1, k], la)
-            sh = jnp.where(hit, table_ref[2, k], sh)
-        coef[0, x] = TIME_STEP * C_NEAR / b
-        coef[1, x] = (TIME_STEP * STIFFNESS * C_NEAR) * la
-        coef[2, x] = (TIME_STEP * STIFFNESS * C_NEAR) * sh
+    peers = n_sta - 1
+    for way in range(8):
+
+        @pl.when(has(way))
+        def _(way=way):
+            pl.semaphore_signal(barrier, inc=1, device_id=device(way), device_id_type=MESH)
+
+        peers = peers + has(way).astype(jnp.int32)
 
     @pl.loop(0, steps)
     def _(n):
@@ -159,56 +164,95 @@
             for x in range(tile_x):
                 weighted[n, c, x] = zero
 
-    for load in loads[6:]:
+    for load in loads:
         load.wait()
-    peers = n_sta - 1
-    for side in range(4):
-        peers = peers + has(side).astype(jnp.int32)
     pl.semaphore_wait(barrier, peers)
 
-    def halo(kind, side, r):
-        axis, step = SIDES[side]
-        at, count = pos[axis]
-        to = jnp.clip(at + step, 0, count - 1)
-        field, edge = ((stress, stress_y), (vel, vel_y))[kind]
-        if axis == "gx":
-            cs = pl.ds(XY if kind == 0 else 0, 3)
-            src = field.at[r, cs, pl.ds(2 if step < 0 else tile_x, 2)]
-            dst = field.at[r, cs, pl.ds(tile_x + 2 if step < 0 else 0, 2)]
+    def part(d, low, high):
+        return low if d < 0 else high
+
+    def mat_copy(way):
+        dx, dy = WAYS[way]
+        if dx:
+            src = mat.at[pl.ds(part(dx, 2, tile_x), 2)]
+            dst = mat.at[pl.ds(part(dx, tile_x + 2, 0), 2)]
         else:
-            at_row = pl.ds(0 if step < 0 else rows - 2, 2)
-            src = field.at[r, pl.ds(0, 3), pl.ds(2, tile_x), at_row]
-            dst = edge.at[r, :, :, at_row]
+            at_row = pl.ds(part(dy, 0, rows - 2), 2)
+            src, dst = mat.at[pl.ds(2, tile_x), at_row], mat_y.at[:, at_row]
         return pltpu.make_async_remote_copy(
             src_ref=src,
             dst_ref=dst,
-            send_sem=h_send.at[kind, side, r],
-            recv_sem=h_recv.at[kind, side, r],
-            device_id={axis: to},
+            send_sem=m_send.at[way],
+            recv_sem=m_recv.at[way],
+            device_id=device(way),
             device_id_type=MESH,
         )
 
-    def send(kind, r):
-        for side in range(4):
-
-            @pl.when(has(side))
-            def _(side=side):
-                halo(kind, side, r).start()
-
-    def arrive(kind, r):
-        for side in range(4):
-
-            @pl.when(has(side ^ 1))
-            def _(side=side):
-                halo(kind, side, r).wait_recv()
-
-            @pl.when(has(side))
-            def _(side=side):
-                halo(kind, side, r).wait_send()
+    def stress_copy(way, r):
+        dx, dy = WAYS[way]
+        if dx:
+            src = stress.at[r, pl.ds(XY, 3), pl.ds(part(dx, 2, tile_x), 2)]
+            dst = stress.at[r, pl.ds(XY, 3), pl.ds(part(dx, tile_x + 2, 0), 2)]
+        else:
+            at_row = pl.ds(part(dy, 0, rows - 2), 2)
+            src = stress.at[r, pl.ds(0, 3), pl.ds(2, tile_x), at_row]
+            dst = stress_y.at[r, :, :, at_row]
+        return pltpu.make_async_remote_copy(
+            src_ref=src,
+            dst_ref=dst,
+            send_sem=i_send.at[way, r],
+            recv_sem=i_recv.at[way, r],
+            device_id=device(way),
+            device_id_type=MESH,
+        )
+
+    def vel_copy(way, p, r):
+        dx, dy = WAYS[way]
+        if dx and dy:
+            at_row = pl.ds(part(dy, 0, rows - 2), 2)
+            src = vel.at[p, r, pl.ds(0, 2), pl.ds(part(dx, 4, tile_x + 2), 2), at_row]
+            dst = vel_y.at[p, r, pl.ds(0, 2), pl.ds(part(dx, tile_x + 2, 0), 2), at_row]
+        elif dx:
+            src = vel.at[p, r, :, pl.ds(part(dx, 4, tile_x), 4)]
+            dst = vel.at[p, r, :, pl.ds(part(dx, tile_x + 4, 0), 4)]
+        else:
+            at_row = pl.ds(part(dy, 0, rows - 4), 4)
+            src = vel.at[p, r, :, pl.ds(4, tile_x), at_row]
+            dst = vel_y.at[p, r, :, pl.ds(2, tile_x), at_row]
+        return pltpu.make_async_remote_copy(
+            src_ref=src,
+            dst_ref=dst,
+            send_sem=h_send.at[p, way, r],
+            recv_sem=h_recv.at[p, way, r],
+            device_id=device(way),
+            device_id_type=MESH,
+        )
+
+    def send(copy, ways, *at):
+        for way in ways:
+
+            @pl.when(has(way))
+            def _(way=way):
+                copy(way, *at).start()
+
+    def arrive(copy, ways, *at):
+        for way in ways:
+
+            @pl.when(has(BACK[way]))
+            def _(way=way):
+                copy(way, *at).wait_recv()
+
+            @pl.when(has(way))
+            def _(way=way):
+                copy(way, *at).wait_send()
+
+    sides, corners = range(4), range(4, 8)
 
     @pl.loop(0, recs)
     def _(r):
-        send(0, r)
+        send(stress_copy, sides, r)
+
+    send(mat_copy, sides)
 
     def row_copy(d):
         to = (sx + d) % n_col
@@ -293,84 +337,153 @@
     band = band + 0.125 * (jnp.where(off == -2, 1.0, 0.0) - jnp.where(off == 2, 1.0, 0.0))
     band = band.astype(BF16)
 
-    def diff_x(ref, r, c, x):
-        near = ref[r, c, x + 3] - ref[r, c, x + 1]
-        return near - 0.125 * (ref[r, c, x + 4] - ref[r, c, x])
-
-    def diff_y(ref, edge, r, c, x):
-        t, e = ref[r, c, x + 2], edge[r, c, x]
+    def diff_x(get, c, x):
+        return (get(c, x + 1) - get(c, x - 1)) - 0.125 * (get(c, x + 2) - get(c, x - 2))
+
+    def diff_y(t, e):
         up1 = pltpu.roll(jnp.where(first1, e, t), rows - 1, 0)
         up2 = pltpu.roll(jnp.where(first2, e, t), rows - 2, 0)
         dn1 = pltpu.roll(jnp.where(last1, e, t), 1, 0)
         dn2 = pltpu.roll(jnp.where(last2, e, t), 2, 0)
         return (up1 - dn1) - 0.125 * (up2 - dn2)
 
-    def diff_z(ref, r, c):
-        f = ref[r, c, pl.ds(2, tile_x)].reshape(tile_x * rows, depth)
+    def diff_z(f):
+        planes = f.shape[0]
+        f = f.reshape(planes * rows, depth)
         hi = f.astype(BF16)
         lo = (f - hi.astype(F32)).astype(BF16)
         both = jnp.concatenate([hi, lo], 1)
         d = jnp.dot(both, band, preferred_element_type=F32)
-        return d.reshape(tile_x, rows, depth)
-
-    def velocity(n, r):
-        zx = diff_z(stress, r, XZ)
-        zy = diff_z(stress, r, YZ)
-        zz = diff_z(stress, r, ZZ)
+        return d.reshape(planes, rows, depth)
+
+    tile = range(tile_x)
+
+    def tables():
+        def look(m, k):
+            v = jnp.zeros((rows, depth), F32)
+            for j in range(table_ref.shape[1]):
+                v = jnp.where(m == j, table_ref[k, j], v)
+            return v
+
+        unit = TIME_STEP * STIFFNESS * C_NEAR
+        for x in range(tile_x + 4):
+            for k in (1, 2):
+                coef[k, x] = unit * look(mat[x], k)
+        for x in tile:
+            for k in (1, 2):
+                coef_y[k - 1, x] = unit * look(mat_y[x], k)
+
+    def buoyancy():
+        for x in tile:
+            m = mat[x + 2]
+            v = jnp.ones((rows, depth), F32)
+            for j in range(table_ref.shape[1]):
+                v = jnp.where(m == j, table_ref[0, j], v)
+            coef[0, x + 2] = TIME_STEP * C_NEAR / v
+
+    def velocity(n, p, r):
+        def s(c, x):
+            return stress[r, c, x + 2]
+
+        def e(c, x):
+            return stress_y[r, c, x]
+
+        zx, zy, zz = (diff_z(stress[r, c, pl.ds(2, tile_x)]) for c in (XZ, YZ, ZZ))
         cell = cell_ref[0, r]
         cx = cell // (n_gy * rows) - gx * tile_x
         cy = cell % (n_gy * rows) - gy * rows
         amp = (AMPLITUDE / C_NEAR) * res_ref[0, r, n]
         spot = jnp.where((row_at == cy) & (lane_at == 0), amp, 0.0)
-        for x in range(tile_x):
-            b = coef[0, x]
-            fx = diff_x(stress, r, XX, x) + diff_y(stress, stress_y, r, XY, x) + zx[x]
-            fy = diff_x(stress, r, XY, x) + diff_y(stress, stress_y, r, YY, x) + zy[x]
-            fz = diff_x(stress, r, XZ, x) + diff_y(stress, stress_y, r, YZ, x) + zz[x]
+        for x in tile:
+            b = coef[0, x + 2]
+            fx = diff_x(s, XX, x) + diff_y(s(XY, x), e(XY, x)) + zx[x]
+            fy = diff_x(s, XY, x) + diff_y(s(YY, x), e(YY, x)) + zy[x]
+            fz = diff_x(s, XZ, x) + diff_y(s(YZ, x), e(YZ, x)) + zz[x]
             fz = fz + spot * jnp.where(cx == x, 1.0, 0.0)
-            vel[r, VX, x + 2] = vel[r, VX, x + 2] + b * fx
-            vel[r, VY, x + 2] = vel[r, VY, x + 2] + b * fy
-            vel[r, VZ, x + 2] = vel[r, VZ, x + 2] + b * fz
-
-    def strain(n, r):
-        zx = diff_z(vel, r, VX)
-        zy = diff_z(vel, r, VY)
-        zz = diff_z(vel, r, VZ)
+            for c, f in ((VX, fx), (VY, fy), (VZ, fz)):
+                vel[p, r, c, x + 4] = vel[1 - p, r, c, x + 4] + b * f
+
+    def strain(n, p, r):
+        def v(c, x):
+            return vel[p, r, c, x + 4]
+
+        def e(c, x):
+            return vel_y[p, r, c, x + 2]
+
+        zx, zy, zz = (diff_z(vel[p, r, c, pl.ds(4, tile_x)]) for c in (VX, VY, VZ))
         res = res_ref[0, r, n]
-        for x in range(tile_x):
-            la, mu = coef[1, x], coef[2, x]
+        for x in tile:
+            la, mu = coef[1, x + 2], coef[2, x + 2]
             mu2 = mu + mu
-            rxx = diff_x(vel, r, VX, x)
-            ryy = diff_y(vel, vel_y, r, VY, x)
+            rxx = diff_x(v, VX, x)
+            ryy = diff_y(v(VY, x), e(VY, x))
             rzz = zz[x]
-            rxy = diff_y(vel, vel_y, r, VX, x) + diff_x(vel, r, VY, x)
-            rxz = zx[x] + diff_x(vel, r, VZ, x)
-            ryz = zy[x] + diff_y(vel, vel_y, r, VZ, x)
+            rxy = diff_y(v(VX, x), e(VX, x)) + diff_x(v, VY, x)
+            rxz = zx[x] + diff_x(v, VZ, x)
+            ryz = zy[x] + diff_y(v(VZ, x), e(VZ, x))
             tr = la * (rxx + ryy + rzz)
             put = ((XX, rxx), (YY, ryy), (ZZ, rzz), (XY, rxy), (XZ, rxz), (YZ, ryz))
-            for k, (c, v) in enumerate(put):
-                weighted[n, k, x] = weighted[n, k, x] + res * v
-                if k < 3:
-                    stress[r, c, x + 2] = stress[r, c, x + 2] + (tr + mu2 * v)
-                else:
-                    stress[r, c, x + 2] = stress[r, c, x + 2] + mu * v
+            for k, (c, d) in enumerate(put):
+                weighted[n, k, x] = weighted[n, k, x] + res * d
+                step = tr + mu2 * d if k < 3 else mu * d
+                stress[r, c, x + 2] = stress[r, c, x + 2] + step
+
+    def strain_edges(p, r):
+        def v(c, x):
+            return vel[p, r, c, x + 4]
+
+        def e(c, x):
+            return vel_y[p, r, c, x + 2]
+
+        for low in (-2, tile_x):
+            zx, zz = (diff_z(vel[p, r, c, pl.ds(low + 4, 2)]) for c in (VX, VZ))
+            for k in range(2):
+                x = low + k
+                la, mu = coef[1, x + 2], coef[2, x + 2]
+                rxx = diff_x(v, VX, x)
+                ryy = diff_y(v(VY, x), e(VY, x))
+                rxy = diff_y(v(VX, x), e(VX, x)) + diff_x(v, VY, x)
+                rxz = zx[k] + diff_x(v, VZ, x)
+                sxx = la * (rxx + ryy + zz[k]) + (mu + mu) * rxx
+                for c, step in ((XX, sxx), (XY, mu * rxy), (XZ, mu * rxz)):
+                    stress[r, c, x + 2] = stress[r, c, x + 2] + step
+        zy, zz = (diff_z(vel_y[p, r, c, pl.ds(2, tile_x)]) for c in (VY, VZ))
+        for x in tile:
+            la, mu = coef_y[0, x], coef_y[1, x]
+            rxx = diff_x(e, VX, x)
+            ryy = diff_y(e(VY, x), v(VY, x))
+            rxy = diff_y(e(VX, x), v(VX, x)) + diff_x(e, VY, x)
+            ryz = zy[x] + diff_y(e(VZ, x), v(VZ, x))
+            syy = la * (rxx + ryy + zz[x]) + (mu + mu) * ryy
+            for c, step in ((YY, syy), (XY, mu * rxy), (YZ, mu * ryz)):
+                stress_y[r, c, x] = stress_y[r, c, x] + step
+
+    buoyancy()
+
+    @pl.loop(0, recs)
+    def _(r):
+        arrive(stress_copy, sides, r)
+        velocity(0, 0, r)
+        send(vel_copy, range(8), 0, r)
+
+    arrive(mat_copy, sides)
+    tables()
 
     @pl.loop(0, steps)
     def _(n):
+        p = n % 2
+
         @pl.loop(0, recs)
         def _(r):
-            arrive(0, r)
-            velocity(n, r)
-            send(1, r)
-
-        @pl.loop(0, recs)
-        def _(r):
-            arrive(1, r)
-            strain(n, r)
+            arrive(vel_copy, sides, p, r)
+            strain(n, p, r)
+            arrive(vel_copy, corners, p, r)
 
             @pl.when(n < steps - 1)
             def _():
-                send(0, r)
+                strain_edges(p, r)
+                velocity(n + 1, 1 - p, r)
+                send(vel_copy, range(8), 1 - p, r)
 
         pl.when(n == 2)(pick_rows)
         pl.when(n == 4)(gather_rows)
@@ -444,11 +557,13 @@
         scratch_shapes=[
             pltpu.VMEM((recs, 6, tile_x + 4, *plane), F32),
             pltpu.VMEM((recs, 3, tile_x, *plane), F32),
-            pltpu.VMEM((recs, 3, tile_x + 4, *plane), F32),
-            pltpu.VMEM((recs, 3, tile_x, *plane), F32),
+            pltpu.VMEM((2, recs, 3, tile_x + 8, *plane), F32),
+            pltpu.VMEM((2, recs, 3, tile_x + 4, *plane), F32),
             pltpu.VMEM((steps, 6, tile_x, *plane), F32),
+            pltpu.VMEM((tile_x + 4, *plane), jnp.int32),
             pltpu.VMEM((tile_x, *plane), jnp.int32),
-            pltpu.VMEM((3, tile_x, *plane), F32),
+            pltpu.VMEM((3, tile_x + 4, *plane), F32),
+            pltpu.VMEM((2, tile_x, *plane), F32),
             pltpu.VMEM((n_col, steps, 6, 2, *plane), BF16),
             pltpu.VMEM((turns * steps, 6, 2, *plane), BF16),
             pltpu.VMEM((turns * steps, 6, 2, *plane), BF16),
@@ -457,8 +572,12 @@
             pltpu.VMEM((n_sta, 2, *plane), F32),
             *[pltpu.SMEM(a.shape, a.dtype) for a in smalls],
             dma((16,)),
-            dma((2, 4, recs)),
-            dma((2, 4, recs)),
+            dma((4,)),
+            dma((4,)),
+            dma((4, recs)),
+            dma((4, recs)),
+            dma((2, 8, recs)),
+            dma((2, 8, recs)),
             dma((n_col - 1,)),
             dma((n_col - 1,)),
             dma((2,)),

time: 72.8 us -> 66.9 us (0.919); the launches traced: 71.7 us -> 66.7 us
  Pallas kernels: 70.4 us -> 65.4 us
    pallas_call x1, Pallas kernels: 70.4 us -> 65.4 us  [local(): pl.pallas_call(body, out_shape=jax.ShapeDtypeStruct((2, 1, *plane), F32),...]
where the time goes in v3:
time: 66.9 us; the launch traced here: 66.7 us
  Pallas kernels  65.4 us (98%)
  local copies, waits for them, and re-layouts  1.3 us (2%)
    pallas_call x1, Pallas kernels, local(): pl.pallas_call(body, out_shape=jax.ShapeDtypeStruct((2, 1, *plane), F32),...  65.4 us

profile of v3, /device:TPU:0, one launch (start us, length us, event | category | flops | bytes accessed | tf_op | source)
XLA Modules:
  0.0 66.7 jit_solution(4032164173399782549)
XLA Ops:
  0.0 65.4 %kernels.1 = f32[2,1,8,128]{3,2,1,0:T(8,128)} custom-call(f32[1,4,9,8,8,128]{5,4,3,2,1,0:T(8,128)} %rec_hbm.1, bf16[1,8,6,8,8,128]{5,4,3,2,1,0:T(8,128)(2,1)} %src_hbm.1, s32[8,8,128]{2,1,0:T(8,128)} %mat_hbm.1, f32[3,16]{1,0:T(4,128)} %bitcast.1, f32[1,4,8]{2,1,0:T(4,128)} %res_hbm.1, s32[1,4]{1,0:T(1,128)} %cell_hbm.1, s32[2,8,8]{2,1,0:T(8,128)} %listed_hbm.1, ...), custom_call_target="tpu_custom_call" | custom-call | tf_op jit(solution)/shard_map/kernels/pallas_call | solution.py:552
  65.4 1.3 %copy.10 = f32[2,1,8,128]{3,2,1,0:T(8,128)} copy(f32[2,1,8,128]{3,2,1,0:T(8,128)} %kernels.1) | data formatting | bytes 16384

commit v4 on v3

--- a/solution.py
+++ b/solution.py
@@ -20,8 +20,9 @@
 YY, YZ, XY, XX, XZ, ZZ = range(6)
 STRESS_FROM = (1, 5, 3, 0, 4, 2)
 VX, VY, VZ = range(3)
-WAYS = ((-1, 0), (1, 0), (0, -1), (0, 1), (-1, -1), (-1, 1), (1, -1), (1, 1))
-BACK = (1, 0, 3, 2, 7, 6, 5, 4)
+WAYS = ((-1, 0), (1, 0), (0, -1), (0, 1), (-1, -1), (-1, 1), (1, -1), (1, 1), (-1, 0), (1, 0))
+BACK = (1, 0, 3, 2, 7, 6, 5, 4, 9, 8)
+FAR = 2
 
 
 def body(
@@ -38,6 +39,8 @@
     stress_y,
     vel,
     vel_y,
+    far_out,
+    far_in,
     weighted,
     mat,
     mat_y,
@@ -63,7 +66,8 @@
     h_recv,
     a_send,
     a_recv,
-    b_sem,
+    b_send,
+    b_recv,
     g_send,
     g_recv,
     r_send,
@@ -129,6 +133,9 @@
                     vel[p, r, c, tile_x + 4 + row] = zero
                 for row in range(tile_x + 4):
                     vel_y[p, r, c, row] = zero
+                for side in range(2):
+                    for k in range(FAR):
+                        far_in[p, r, side, c, k] = zero.astype(BF16)
 
     barrier = pltpu.get_barrier_semaphore()
 
@@ -145,11 +152,10 @@
         dx, dy = WAYS[way]
         return {"gx": jnp.clip(gx + dx, 0, n_gx - 1), "gy": jnp.clip(gy + dy, 0, n_gy - 1)}
 
-    for d in range(1, n_sta):
-        pl.semaphore_signal(
-            barrier, inc=1, device_id={"sta": (sta + d) % n_sta}, device_id_type=MESH
-        )
-    peers = n_sta - 1
+    column = [2 * ((sx + d) % n_col) + sy for d in range(1, n_col)] + [2 * sx + 1 - sy]
+    for to in column:
+        pl.semaphore_signal(barrier, inc=1, device_id={"sta": to}, device_id_type=MESH)
+    peers = len(column)
     for way in range(8):
 
         @pl.when(has(way))
@@ -212,9 +218,12 @@
             at_row = pl.ds(part(dy, 0, rows - 2), 2)
             src = vel.at[p, r, pl.ds(0, 2), pl.ds(part(dx, 4, tile_x + 2), 2), at_row]
             dst = vel_y.at[p, r, pl.ds(0, 2), pl.ds(part(dx, tile_x + 2, 0), 2), at_row]
+        elif way >= 8:
+            src = far_out.at[p, r, way - 8]
+            dst = far_in.at[p, r, way - 8]
         elif dx:
-            src = vel.at[p, r, :, pl.ds(part(dx, 4, tile_x), 4)]
-            dst = vel.at[p, r, :, pl.ds(part(dx, tile_x + 4, 0), 4)]
+            src = vel.at[p, r, :, pl.ds(part(dx, 4, tile_x + 2), 2)]
+            dst = vel.at[p, r, :, pl.ds(part(dx, tile_x + 4, 2), 2)]
         else:
             at_row = pl.ds(part(dy, 0, rows - 4), 4)
             src = vel.at[p, r, :, pl.ds(4, tile_x), at_row]
@@ -246,7 +255,8 @@
             def _(way=way):
                 copy(way, *at).wait_send()
 
-    sides, corners = range(4), range(4, 8)
+    edges, corners, all_ways = (8, 9, 0, 1, 2, 3), range(4, 8), (8, 9, *range(8))
+    sides = range(4)
 
     @pl.loop(0, recs)
     def _(r):
@@ -268,64 +278,65 @@
     for d in range(1, n_col):
         row_copy(d).start()
 
-    partner_copy = pltpu.make_async_remote_copy(
-        src_ref=mine,
-        dst_ref=other,
-        send_sem=b_sem.at[0],
-        recv_sem=b_sem.at[1],
-        device_id={"sta": 2 * sx + 1 - sy},
-        device_id_type=MESH,
-    )
-
-    def ring(k):
+    def piece(q):
+        return pltpu.make_async_remote_copy(
+            src_ref=mine.at[q],
+            dst_ref=other.at[q],
+            send_sem=b_send.at[q],
+            recv_sem=b_recv.at[q],
+            device_id={"sta": 2 * sx + 1 - sy},
+            device_id_type=MESH,
+        )
+
+    def ring(k, t):
         step = 1 if k % 2 == 0 else n_col - 1
         to = (sx + step) % n_col
         slot = sx if k < 2 else (sx + n_col - step) % n_col
-        part = pl.ds(0, turns * steps) if k < 2 else pl.ds((k - 2) * steps, steps)
-        ref = gath.at[slot, part]
+        half = steps // 2
+        begin, size = (0, steps) if k < 2 else ((k - 2) * half, half)
+        ref = gath.at[slot, pl.ds(t * steps + begin, size)]
         return pltpu.make_async_remote_copy(
             src_ref=ref,
             dst_ref=ref,
-            send_sem=g_send.at[k],
-            recv_sem=g_recv.at[k],
+            send_sem=g_send.at[k, t],
+            recv_sem=g_recv.at[k, t],
             device_id={"sta": 2 * to + sy},
             device_id_type=MESH,
         )
 
-    def pick_rows():
+    def take_rows():
         own_rows.wait()
         for d in range(1, n_col):
             row_copy(d).wait()
-        for t in range(turns):
-
-            @pl.loop(0, steps)
-            def _(n, t=t):
-                p = pick_ref[t, n]
-                keep = p % 2 == sy
-                for c in range(6):
-                    for j in range(2):
-                        v = rows_in[p // 2, n, c, j]
-                        mine[t * steps + n, c, j] = jnp.where(keep, v, jnp.zeros_like(v))
-
-        partner_copy.start()
-
-    def gather_rows():
-        partner_copy.wait()
-
-        @pl.loop(0, turns * steps)
-        def _(q):
+
+    def pick_piece(q):
+        m = q % steps
+        p = pick_ref[q // steps, m]
+        keep = p % 2 == sy
+        for c in range(6):
+            for j in range(2):
+                v = rows_in[p // 2, m, c, j]
+                mine[q, c, j] = jnp.where(keep, v, jnp.zeros_like(v))
+        piece(q).start()
+
+    def gather_rows(t):
+        @pl.loop(0, steps)
+        def _(m):
+            q = t * steps + m
+            piece(q).wait()
             for c in range(6):
                 for j in range(2):
                     gath[sx, q, c, j] = mine[q, c, j] + other[q, c, j]
 
-        ring(0).start()
-        ring(1).start()
-
-    def relay_rows():
-        ring(0).wait()
-        ring(1).wait()
-        ring(2).start()
-        ring(3).start()
+        ring(0, t).start()
+        ring(1, t).start()
+
+    def relay_rows(t):
+        for k in range(4):
+            if k < 2:
+                ring(k, t).wait()
+            else:
+                ring(k, t).start()
 
     row_at = lax.broadcasted_iota(jnp.int32, (rows, depth), 0)
     lane_at = lax.broadcasted_iota(jnp.int32, (rows, depth), 1)
@@ -402,6 +413,16 @@
             fz = fz + spot * jnp.where(cx == x, 1.0, 0.0)
             for c, f in ((VX, fx), (VY, fy), (VZ, fz)):
                 vel[p, r, c, x + 4] = vel[1 - p, r, c, x + 4] + b * f
+        for c in range(3):
+            for side, (first, way) in enumerate(((6, 1), (tile_x + 1, -1))):
+                for k in range(FAR):
+                    far_out[p, r, side, c, k] = vel[p, r, c, first + way * k].astype(BF16)
+
+    def unpack(p, r):
+        for c in range(3):
+            for side, (first, way) in enumerate(((tile_x + 6, 1), (1, -1))):
+                for k in range(FAR):
+                    vel[p, r, c, first + way * k] = far_in[p, r, side, c, k].astype(F32)
 
     def strain(n, p, r):
         def v(c, x):
@@ -459,12 +480,13 @@
                 stress_y[r, c, x] = stress_y[r, c, x] + step
 
     buoyancy()
+    first_piece = 2
 
     @pl.loop(0, recs)
     def _(r):
         arrive(stress_copy, sides, r)
         velocity(0, 0, r)
-        send(vel_copy, range(8), 0, r)
+        send(vel_copy, all_ways, 0, r)
 
     arrive(mat_copy, sides)
     tables()
@@ -472,10 +494,12 @@
     @pl.loop(0, steps)
     def _(n):
         p = n % 2
+        pl.when(n == first_piece)(take_rows)
 
         @pl.loop(0, recs)
         def _(r):
-            arrive(vel_copy, sides, p, r)
+            arrive(vel_copy, edges, p, r)
+            unpack(p, r)
             strain(n, p, r)
             arrive(vel_copy, corners, p, r)
 
@@ -483,14 +507,20 @@
             def _():
                 strain_edges(p, r)
                 velocity(n + 1, 1 - p, r)
-                send(vel_copy, range(8), 1 - p, r)
-
-        pl.when(n == 2)(pick_rows)
-        pl.when(n == 4)(gather_rows)
-        pl.when(n == 6)(relay_rows)
-
-    ring(2).wait()
-    ring(3).wait()
+                send(vel_copy, all_ways, 1 - p, r)
+
+            @pl.when((n >= first_piece) & (n < first_piece + turns))
+            def _():
+                for j in range(steps // recs):
+                    pick_piece((n - first_piece) * steps + r * (steps // recs) + j)
+
+        for t in range(turns):
+            pl.when(n == first_piece + 1 + t)(functools.partial(gather_rows, t))
+            pl.when(n == first_piece + 3 + t)(functools.partial(relay_rows, t))
+
+    for t in range(turns):
+        ring(2, t).wait()
+        ring(3, t).wait()
 
     for x in range(tile_x):
         for k in range(2):
@@ -559,6 +589,8 @@
             pltpu.VMEM((recs, 3, tile_x, *plane), F32),
             pltpu.VMEM((2, recs, 3, tile_x + 8, *plane), F32),
             pltpu.VMEM((2, recs, 3, tile_x + 4, *plane), F32),
+            pltpu.VMEM((2, recs, 2, 3, FAR, *plane), BF16),
+            pltpu.VMEM((2, recs, 2, 3, FAR, *plane), BF16),
             pltpu.VMEM((steps, 6, tile_x, *plane), F32),
             pltpu.VMEM((tile_x + 4, *plane), jnp.int32),
             pltpu.VMEM((tile_x, *plane), jnp.int32),
@@ -576,13 +608,14 @@
             dma((4,)),
             dma((4, recs)),
             dma((4, recs)),
-            dma((2, 8, recs)),
-            dma((2, 8, recs)),
+            dma((2, 10, recs)),
+            dma((2, 10, recs)),
             dma((n_col - 1,)),
             dma((n_col - 1,)),
-            dma((2,)),
-            dma((4,)),
-            dma((4,)),
+            dma((turns * steps,)),
+            dma((turns * steps,)),
+            dma((4, turns)),
+            dma((4, turns)),
             dma((n_sta,)),
             dma((n_sta,)),
         ],

time: 66.9 us -> 59.3 us (0.89)
  Pallas kernels: 65.4 us -> 57.5 us
    pallas_call x1, Pallas kernels: 65.4 us -> 57.5 us  [local(): pl.pallas_call(body, out_shape=jax.ShapeDtypeStruct((2, 1, *plane), F32),...]
where the time goes in v4:
time: 59.3 us; the launch traced here: 58.8 us
  Pallas kernels  57.5 us (97%)
  local copies, waits for them, and re-layouts  1.3 us (2%)
    pallas_call x1, Pallas kernels, local(): pl.pallas_call(body, out_shape=jax.ShapeDtypeStruct((2, 1, *plane), F32),...  57.5 us
    unnamed x1, local copies, waits for them, and re-layouts  1.3 us

profile of v4, /device:TPU:0, one launch (start us, length us, event | category | flops | bytes accessed | tf_op | source)
XLA Modules:
  0.0 58.8 jit_solution(15087377143633583011)
XLA Ops:
  0.0 57.5 %kernels.1 = f32[2,1,8,128]{3,2,1,0:T(8,128)} custom-call(f32[1,4,9,8,8,128]{5,4,3,2,1,0:T(8,128)} %rec_hbm.1, bf16[1,8,6,8,8,128]{5,4,3,2,1,0:T(8,128)(2,1)} %src_hbm.1, s32[8,8,128]{2,1,0:T(8,128)} %mat_hbm.1, f32[3,16]{1,0:T(4,128)} %bitcast.1, f32[1,4,8]{2,1,0:T(4,128)} %res_hbm.1, s32[1,4]{1,0:T(1,128)} %cell_hbm.1, s32[2,8,8]{2,1,0:T(8,128)} %listed_hbm.1, ...), custom_call_target="tpu_custom_call" | custom-call | tf_op jit(solution)/shard_map/kernels/pallas_call | solution.py:582
  57.5 1.3 %copy.10 = f32[2,1,8,128]{3,2,1,0:T(8,128)} copy(f32[2,1,8,128]{3,2,1,0:T(8,128)} %kernels.1) | data formatting | bytes 16384

commit v5 on v4

--- a/solution.py
+++ b/solution.py
@@ -255,8 +255,7 @@
             def _(way=way):
                 copy(way, *at).wait_send()
 
-    edges, corners, all_ways = (8, 9, 0, 1, 2, 3), range(4, 8), (8, 9, *range(8))
-    sides = range(4)
+    sides, outer, all_ways = range(4), (8, 9, 4, 5, 6, 7), (4, 5, 6, 7, 0, 1, 2, 3, 8, 9)
 
     @pl.loop(0, recs)
     def _(r):
@@ -288,13 +287,15 @@
             device_id_type=MESH,
         )
 
+    chunk = 4
+
     def ring(k, t):
         step = 1 if k % 2 == 0 else n_col - 1
         to = (sx + step) % n_col
         slot = sx if k < 2 else (sx + n_col - step) % n_col
-        half = steps // 2
-        begin, size = (0, steps) if k < 2 else ((k - 2) * half, half)
-        ref = gath.at[slot, pl.ds(t * steps + begin, size)]
+        half = chunk // 2
+        begin, size = (0, chunk) if k < 2 else ((k - 2) * half, half)
+        ref = gath.at[slot, pl.ds(t * chunk + begin, size)]
         return pltpu.make_async_remote_copy(
             src_ref=ref,
             dst_ref=ref,
@@ -320,9 +321,8 @@
         piece(q).start()
 
     def gather_rows(t):
-        @pl.loop(0, steps)
-        def _(m):
-            q = t * steps + m
+        @pl.loop(t * chunk, (t + 1) * chunk)
+        def _(q):
             piece(q).wait()
             for c in range(6):
                 for j in range(2):
@@ -480,7 +480,7 @@
                 stress_y[r, c, x] = stress_y[r, c, x] + step
 
     buoyancy()
-    first_piece = 2
+    chunks = turns * steps // chunk
 
     @pl.loop(0, recs)
     def _(r):
@@ -494,31 +494,33 @@
     @pl.loop(0, steps)
     def _(n):
         p = n % 2
-        pl.when(n == first_piece)(take_rows)
-
         @pl.loop(0, recs)
         def _(r):
-            arrive(vel_copy, edges, p, r)
-            unpack(p, r)
+            arrive(vel_copy, sides, p, r)
             strain(n, p, r)
-            arrive(vel_copy, corners, p, r)
+            arrive(vel_copy, outer, p, r)
 
             @pl.when(n < steps - 1)
             def _():
+                unpack(p, r)
                 strain_edges(p, r)
                 velocity(n + 1, 1 - p, r)
                 send(vel_copy, all_ways, 1 - p, r)
 
-            @pl.when((n >= first_piece) & (n < first_piece + turns))
-            def _():
-                for j in range(steps // recs):
-                    pick_piece((n - first_piece) * steps + r * (steps // recs) + j)
-
-        for t in range(turns):
-            pl.when(n == first_piece + 1 + t)(functools.partial(gather_rows, t))
-            pl.when(n == first_piece + 3 + t)(functools.partial(relay_rows, t))
-
-    for t in range(turns):
+            for t in range(chunks):
+                pl.when((n == t + 2) & (r == 1))(functools.partial(gather_rows, t))
+
+        pl.when(n == 0)(take_rows)
+
+        @pl.when(n < chunks)
+        def _():
+            for j in range(chunk):
+                pick_piece(n * chunk + j)
+
+        for t in range(chunks):
+            pl.when(n == t + 3)(functools.partial(relay_rows, t))
+
+    for t in range(chunks):
         ring(2, t).wait()
         ring(3, t).wait()
 
@@ -614,8 +616,8 @@
             dma((n_col - 1,)),
             dma((turns * steps,)),
             dma((turns * steps,)),
-            dma((4, turns)),
-            dma((4, turns)),
+            dma((4, turns * steps // 4)),
+            dma((4, turns * steps // 4)),
             dma((n_sta,)),
             dma((n_sta,)),
         ],

time: 59.3 us -> 56.2 us (0.948)
  Pallas kernels: 57.5 us -> 53.9 us
    pallas_call x1, Pallas kernels: 57.5 us -> 53.9 us  [local(): pl.pallas_call(body, out_shape=jax.ShapeDtypeStruct((2, 1, *plane), F32),...]
where the time goes in v5:
time: 56.2 us; the launch traced here: 55.2 us
  Pallas kernels  53.9 us (96%)
  local copies, waits for them, and re-layouts  1.3 us (2%)
    pallas_call x1, Pallas kernels, local(): pl.pallas_call(body, out_shape=jax.ShapeDtypeStruct((2, 1, *plane), F32),...  53.9 us
    unnamed x1, local copies, waits for them, and re-layouts  1.3 us

profile of v5, /device:TPU:0, one launch (start us, length us, event | category | flops | bytes accessed | tf_op | source)
XLA Modules:
  0.0 55.2 jit_solution(7642794852706461978)
XLA Ops:
  0.0 53.9 %kernels.1 = f32[2,1,8,128]{3,2,1,0:T(8,128)} custom-call(f32[1,4,9,8,8,128]{5,4,3,2,1,0:T(8,128)} %rec_hbm.1, bf16[1,8,6,8,8,128]{5,4,3,2,1,0:T(8,128)(2,1)} %src_hbm.1, s32[8,8,128]{2,1,0:T(8,128)} %mat_hbm.1, f32[3,16]{1,0:T(4,128)} %bitcast.1, f32[1,4,8]{2,1,0:T(4,128)} %res_hbm.1, s32[1,4]{1,0:T(1,128)} %cell_hbm.1, s32[2,8,8]{2,1,0:T(8,128)} %listed_hbm.1, ...), custom_call_target="tpu_custom_call" | custom-call | tf_op jit(solution)/shard_map/kernels/pallas_call | solution.py:584
  53.9 1.3 %copy.10 = f32[2,1,8,128]{3,2,1,0:T(8,128)} copy(f32[2,1,8,128]{3,2,1,0:T(8,128)} %kernels.1) | data formatting | bytes 16384

commit v6 on v5

--- a/solution.py
+++ b/solution.py
@@ -41,6 +41,8 @@
     vel_y,
     far_out,
     far_in,
+    cor_out,
+    cor_in,
     weighted,
     mat,
     mat_y,
@@ -121,6 +123,9 @@
 
     @pl.loop(0, recs)
     def _(r):
+        for p in range(2):
+            for k in range(4):
+                cor_in[p, r, k] = zero.astype(BF16)
         for c in range(6):
             for row in (0, 1, tile_x + 2, tile_x + 3):
                 stress[r, c, row] = zero
@@ -215,9 +220,7 @@
     def vel_copy(way, p, r):
         dx, dy = WAYS[way]
         if dx and dy:
-            at_row = pl.ds(part(dy, 0, rows - 2), 2)
-            src = vel.at[p, r, pl.ds(0, 2), pl.ds(part(dx, 4, tile_x + 2), 2), at_row]
-            dst = vel_y.at[p, r, pl.ds(0, 2), pl.ds(part(dx, tile_x + 2, 0), 2), at_row]
+            src, dst = cor_out.at[p, r, way - 4], cor_in.at[p, r, way - 4]
         elif way >= 8:
             src = far_out.at[p, r, way - 8]
             dst = far_in.at[p, r, way - 8]
@@ -255,6 +258,7 @@
             def _(way=way):
                 copy(way, *at).wait_send()
 
+    corners = range(4, 8)
     sides, outer, all_ways = range(4), (8, 9, 4, 5, 6, 7), (4, 5, 6, 7, 0, 1, 2, 3, 8, 9)
 
     @pl.loop(0, recs)
@@ -418,13 +422,29 @@
                 for k in range(FAR):
                     far_out[p, r, side, c, k] = vel[p, r, c, first + way * k].astype(BF16)
 
+        for way in corners:
+            dx, dy = WAYS[way]
+            got = None
+            for k in range(4):
+                f = vel[p, r, k // 2, part(dx, 4, tile_x + 2) + k % 2]
+                shift = (2 * k + part(dy, 0, 2)) % rows
+                f = pltpu.roll(f, shift, 0) if shift else f
+                got = f if got is None else jnp.where(row_at >= 2 * k, f, got)
+            cor_out[p, r, way - 4] = got.astype(BF16)
+
     def unpack(p, r):
+        for low, high, first in ((6, 7, 0), (4, 5, tile_x + 2)):
+            a, b = cor_in[p, r, low - 4].astype(F32), cor_in[p, r, high - 4].astype(F32)
+            for k in range(4):
+                fa = pltpu.roll(a, rows - 2 * k, 0) if k else a
+                fb = pltpu.roll(b, rows - 2 - 2 * k, 0) if k < 3 else b
+                vel_y[p, r, k // 2, first + k % 2] = jnp.where(row_at < 2, fa, fb)
         for c in range(3):
             for side, (first, way) in enumerate(((tile_x + 6, 1), (1, -1))):
                 for k in range(FAR):
                     vel[p, r, c, first + way * k] = far_in[p, r, side, c, k].astype(F32)
 
-    def strain(n, p, r):
+    def strain(n, p, r, res, last):
         def v(c, x):
             return vel[p, r, c, x + 4]
 
@@ -432,7 +452,6 @@
             return vel_y[p, r, c, x + 2]
 
         zx, zy, zz = (diff_z(vel[p, r, c, pl.ds(4, tile_x)]) for c in (VX, VY, VZ))
-        res = res_ref[0, r, n]
         for x in tile:
             la, mu = coef[1, x + 2], coef[2, x + 2]
             mu2 = mu + mu
@@ -445,6 +464,9 @@
             tr = la * (rxx + ryy + rzz)
             put = ((XX, rxx), (YY, ryy), (ZZ, rzz), (XY, rxy), (XZ, rxz), (YZ, ryz))
             for k, (c, d) in enumerate(put):
+                if last:
+                    weighted[n, k, x] = d
+                    continue
                 weighted[n, k, x] = weighted[n, k, x] + res * d
                 step = tr + mu2 * d if k < 3 else mu * d
                 stress[r, c, x + 2] = stress[r, c, x + 2] + step
@@ -491,20 +513,21 @@
     arrive(mat_copy, sides)
     tables()
 
-    @pl.loop(0, steps)
+    @pl.loop(0, steps - 1)
     def _(n):
         p = n % 2
+
         @pl.loop(0, recs)
         def _(r):
             arrive(vel_copy, sides, p, r)
-            strain(n, p, r)
+            strain(n, p, r, res_ref[0, r, n], False)
             arrive(vel_copy, outer, p, r)
-
-            @pl.when(n < steps - 1)
+            unpack(p, r)
+            strain_edges(p, r)
+            velocity(n + 1, 1 - p, r)
+
+            @pl.when(n < steps - 2)
             def _():
-                unpack(p, r)
-                strain_edges(p, r)
-                velocity(n + 1, 1 - p, r)
                 send(vel_copy, all_ways, 1 - p, r)
 
             for t in range(chunks):
@@ -517,12 +540,18 @@
             for j in range(chunk):
                 pick_piece(n * chunk + j)
 
-        for t in range(chunks):
+        for t in range(chunks - 1):
             pl.when(n == t + 3)(functools.partial(relay_rows, t))
 
-    for t in range(chunks):
-        ring(2, t).wait()
-        ring(3, t).wait()
+    end = (steps - 1) % 2
+    for c in range(3):
+        for x in tile:
+            total = res_ref[0, 0, steps - 1] * vel[end, 0, c, x + 4]
+            for r in range(1, recs):
+                total = total + res_ref[0, r, steps - 1] * vel[end, r, c, x + 4]
+            vel[end, 0, c, x + 4] = total
+    send(vel_copy, sides, end, 0)
+    relay_rows(chunks - 1)
 
     for x in range(tile_x):
         for k in range(2):
@@ -530,8 +559,7 @@
 
     scale = KERNEL_SCALE * C_NEAR
 
-    @pl.loop(0, steps)
-    def _(n):
+    def correlate(n):
         share = [listed_ref[t, n, sta].astype(F32) for t in range(turns)]
         for x in range(tile_x):
             comb = []
@@ -548,6 +576,19 @@
                 mu = mu + comb[c] * w[c]
             acc[x, 0] = acc[x, 0] + scale * lam
             acc[x, 1] = acc[x, 1] + (2.0 * scale) * mu
+
+    def landed(t):
+        ring(2, t).wait()
+        ring(3, t).wait()
+
+    early = steps // 2
+    for t in range(chunks - 1):
+        landed(t)
+    pl.loop(0, early)(correlate)
+    arrive(vel_copy, sides, end, 0)
+    strain(steps - 1, end, 0, None, True)
+    landed(chunks - 1)
+    pl.loop(early, steps)(correlate)
 
     def share_copy(d):
         to = (sta + d) % n_sta
@@ -593,6 +634,8 @@
             pltpu.VMEM((2, recs, 3, tile_x + 4, *plane), F32),
             pltpu.VMEM((2, recs, 2, 3, FAR, *plane), BF16),
             pltpu.VMEM((2, recs, 2, 3, FAR, *plane), BF16),
+            pltpu.VMEM((2, recs, 4, *plane), BF16),
+            pltpu.VMEM((2, recs, 4, *plane), BF16),
             pltpu.VMEM((steps, 6, tile_x, *plane), F32),
             pltpu.VMEM((tile_x + 4, *plane), jnp.int32),
             pltpu.VMEM((tile_x, *plane), jnp.int32),

time: 56.2 us -> 55.3 us (0.984)
  Pallas kernels: 53.9 us -> 53.3 us
    pallas_call x1, Pallas kernels: 53.9 us -> 53.3 us  [local(): pl.pallas_call(body, out_shape=jax.ShapeDtypeStruct((2, 1, *plane), F32),...]
where the time goes in v6:
time: 55.3 us; the launch traced here: 54.6 us
  Pallas kernels  53.3 us (96%)
  local copies, waits for them, and re-layouts  1.3 us (2%)
    pallas_call x1, Pallas kernels, local(): pl.pallas_call(body, out_shape=jax.ShapeDtypeStruct((2, 1, *plane), F32),...  53.3 us
    unnamed x1, local copies, waits for them, and re-layouts  1.3 us

profile of v6, /device:TPU:0, one launch (start us, length us, event | category | flops | bytes accessed | tf_op | source)
XLA Modules:
  0.0 54.6 jit_solution(8999682067163499568)
XLA Ops:
  0.0 53.3 %kernels.1 = f32[2,1,8,128]{3,2,1,0:T(8,128)} custom-call(f32[1,4,9,8,8,128]{5,4,3,2,1,0:T(8,128)} %rec_hbm.1, bf16[1,8,6,8,8,128]{5,4,3,2,1,0:T(8,128)(2,1)} %src_hbm.1, s32[8,8,128]{2,1,0:T(8,128)} %mat_hbm.1, f32[3,16]{1,0:T(4,128)} %bitcast.1, f32[1,4,8]{2,1,0:T(4,128)} %res_hbm.1, s32[1,4]{1,0:T(1,128)} %cell_hbm.1, s32[2,8,8]{2,1,0:T(8,128)} %listed_hbm.1, ...), custom_call_target="tpu_custom_call" | custom-call | tf_op jit(solution)/shard_map/kernels/pallas_call | solution.py:625
  53.3 1.3 %copy.10 = f32[2,1,8,128]{3,2,1,0:T(8,128)} copy(f32[2,1,8,128]{3,2,1,0:T(8,128)} %kernels.1) | data formatting | bytes 16384

commit v7 on v6

--- a/solution.py
+++ b/solution.py
@@ -601,11 +601,12 @@
             device_id_type=MESH,
         )
 
-    for d in range(1, n_sta):
+    far_first = sorted(range(1, n_sta), key=lambda d: abs(d - n_sta // 2))
+    for d in far_first:
         share_copy(d).start()
     for k in range(2):
         out_ref[k, 0] = acc[sta, k]
-    for d in range(1, n_sta):
+    for d in reversed(far_first):
         share_copy(d).wait()
         for k in range(2):
             out_ref[k, 0] = out_ref[k, 0] + parts[d, k]

time: 55.3 us -> 55.1 us (level)
  no operation moved by 1% of the time
where the time goes in v7:
time: 55.1 us; the launch traced here: 54.5 us
  Pallas kernels  53.2 us (97%)
  local copies, waits for them, and re-layouts  1.3 us (2%)
    pallas_call x1, Pallas kernels, local(): pl.pallas_call(body, out_shape=jax.ShapeDtypeStruct((2, 1, *plane), F32),...  53.2 us
    unnamed x1, local copies, waits for them, and re-layouts  1.3 us

profile of v7, /device:TPU:0, one launch (start us, length us, event | category | flops | bytes accessed | tf_op | source)
XLA Modules:
  0.0 54.5 jit_solution(16597884164446134591)
XLA Ops:
  0.0 53.2 %kernels.1 = f32[2,1,8,128]{3,2,1,0:T(8,128)} custom-call(f32[1,4,9,8,8,128]{5,4,3,2,1,0:T(8,128)} %rec_hbm.1, bf16[1,8,6,8,8,128]{5,4,3,2,1,0:T(8,128)(2,1)} %src_hbm.1, s32[8,8,128]{2,1,0:T(8,128)} %mat_hbm.1, f32[3,16]{1,0:T(4,128)} %bitcast.1, f32[1,4,8]{2,1,0:T(4,128)} %res_hbm.1, s32[1,4]{1,0:T(1,128)} %cell_hbm.1, s32[2,8,8]{2,1,0:T(8,128)} %listed_hbm.1, ...), custom_call_target="tpu_custom_call" | custom-call | tf_op jit(solution)/shard_map/kernels/pallas_call | solution.py:626
  53.2 1.3 %copy.10 = f32[2,1,8,128]{3,2,1,0:T(8,128)} copy(f32[2,1,8,128]{3,2,1,0:T(8,128)} %kernels.1) | data formatting | bytes 16384
